TPU v7x, 512 devices: a whole 4x8x8 slice. The times are simulated.
512 devices in a mesh: row: 8 (over x, y_hi), col: 8 (over y_lo, core), scan: 8 (over z).
Axes of the slice: x: 4, y: 8 (y_hi: 2, y_lo: 4; y = y_hi * 4 + y_lo), z: 8, core: 2. Of those that a mesh axis runs over, the one named last changes fastest.
Arguments:
- object_field: float32 [2, 2, 4096, 4096], P(None, None, 'row', 'col'), may hold values from -6 to 6
- probe_field: float32 [2, 256, 256], replicated, may hold values from -6 to 6
- prop_phase: float32 [256, 256], replicated, may hold values from -3.140625 to 3.140625
- measured: float32 [8, 8, 8, 3, 256, 256], P('row', 'col', 'scan'), may hold values from 0.3 to 3
- positions: int32 [8, 8, 8, 3, 2], P('row', 'col', 'scan'), may hold values from -64 to 320, as said below
- counts: int32 [8, 8, 8], P('row', 'col', 'scan'), may hold values from 1 to 3, as said below
Outputs:
- object_grad: float32 [2, 2, 4096, 4096], P(None, None, ('row', 'scan'), 'col')
Inputs may be any that keep to these rules, and one draw needn't show every extreme that they name: `positions`: every patch lies inside the object; slots at and past the device's count are unused. `counts`: loads are uneven: some devices hold 3 patches while others of the same tile hold one.
All inputs are finite; a program needn't handle non-finite values.
Results may differ from a plain program's by a relative error of at most 0.018.
Values sent between devices are 32-bit elements; how exact they have to be, the bound alone decides.
A program may use at most 64 MiB of HBM per device.

v0:
```python
import math

import jax
import jax.numpy as jnp
from jax import lax
from jax.sharding import PartitionSpec as P

PATCH = 256
HALO = 64
PMAX = 3


def from_behind(block, axis, distance):
    devices = range(lax.axis_size(axis))
    route = [(i - distance, i) for i in devices if i - distance in devices]
    return lax.ppermute(block, axis, route)


def extended_2(array, sides, width):
    for axis, dim in sides:
        size, length = (lax.axis_size(axis), array.shape[dim])
        up = [(i, (i + 1) % size) for i in range(size - 1)]
        down = [(j, i) for i, j in up]
        last = lax.slice_in_dim(array, length - width, length, axis=dim)
        first = lax.slice_in_dim(array, 0, width, axis=dim)
        before = lax.ppermute(last, axis, up)
        after = lax.ppermute(first, axis, down)
        array = jnp.concatenate([before, array, after], axis=dim)
    return array


def dft_tables(length):
    index_line = jnp.arange(length, dtype=jnp.int32)
    product = index_line[:, None] * index_line[None, :] % length
    angles = product.astype(jnp.float32) * (2.0 * math.pi / length)
    cosines = jnp.cos(angles) / math.sqrt(length)
    sines = jnp.sin(angles) / math.sqrt(length)
    left_fwd = jnp.stack([jnp.stack([cosines, sines], 1), jnp.stack([-sines, cosines], 1)], 0)
    right_fwd = jnp.stack([jnp.stack([cosines, -sines], 1), jnp.stack([sines, cosines], 1)], 0)
    left_inv = jnp.stack([jnp.stack([cosines, -sines], 1), jnp.stack([sines, cosines], 1)], 0)
    right_inv = jnp.stack([jnp.stack([cosines, sines], 1), jnp.stack([-sines, cosines], 1)], 0)
    return (
        left_fwd.astype(jnp.bfloat16),
        right_fwd.astype(jnp.bfloat16),
        left_inv.astype(jnp.bfloat16),
        right_inv.astype(jnp.bfloat16),
    )


def transform(values, left_table, right_table):
    middle = jnp.einsum("qapb,pbc->qac", left_table, values, preferred_element_type=jnp.float32)
    middle = middle.astype(jnp.bfloat16)
    return jnp.einsum("pab,pbqc->qac", middle, right_table, preferred_element_type=jnp.float32)


def complex_mul(first, second):
    return jnp.stack(
        [first[0] * second[0] - first[1] * second[1], first[0] * second[1] + first[1] * second[0]]
    )


def conj_mul(first, second):
    return jnp.stack(
        [first[0] * second[0] + first[1] * second[1], first[0] * second[1] - first[1] * second[0]]
    )


def patch_grads(first_slice, second_slice, probe_field, propagator, intensity, tables):
    left_fwd, right_fwd, left_inv, right_inv = tables
    entrance = complex_mul(probe_field, first_slice).astype(jnp.bfloat16)
    spectrum = complex_mul(propagator, transform(entrance, left_fwd, right_fwd)).astype(
        jnp.bfloat16
    )
    arrived = transform(spectrum, left_inv, right_inv)
    leaving = complex_mul(second_slice, arrived).astype(jnp.bfloat16)
    far_field = transform(leaving, left_fwd, right_fwd)
    power = far_field[0] * far_field[0] + far_field[1] * far_field[1]
    residual = ((power - intensity)[None] * far_field).astype(jnp.bfloat16)
    back_second = transform(residual, left_inv, right_inv)
    grad_second = conj_mul(arrived, back_second)
    through = conj_mul(second_slice, back_second).astype(jnp.bfloat16)
    back_spectrum = conj_mul(propagator, transform(through, left_fwd, right_fwd)).astype(
        jnp.bfloat16
    )
    back_first = transform(back_spectrum, left_inv, right_inv)
    grad_first = conj_mul(probe_field, back_first)
    return jnp.stack([grad_first, grad_second])


def pass_rows(strip, offset):
    return from_behind(strip, "row", offset)


def pass_cols(strip, offset):
    return from_behind(strip, "col", offset)


def fold_rows(gradient, tile_size):
    top_rim = gradient[:, :HALO]
    bottom_rim = gradient[:, tile_size + HALO :]
    core_rows = gradient[:, HALO : tile_size + HALO]
    core_rows = core_rows.at[:, :HALO].add(pass_rows(bottom_rim, 1))
    return core_rows.at[:, tile_size - HALO :].add(pass_rows(top_rim, -1))


def fold_cols(gradient, tile_size):
    left_rim = gradient[:, :, :HALO]
    right_rim = gradient[:, :, tile_size + HALO :]
    core_cols = gradient[:, :, HALO : tile_size + HALO]
    core_cols = core_cols.at[:, :, :HALO].add(pass_cols(right_rim, 1))
    return core_cols.at[:, :, tile_size - HALO :].add(pass_cols(left_rim, -1))


def shards(object_field, probe_field, prop_phase, measured, positions, counts):
    tile_size = object_field.shape[2]
    extended = extended_2(object_field, (("row", 2), ("col", 3)), HALO)
    tables = dft_tables(PATCH)
    propagator = jnp.stack([jnp.cos(prop_phase), jnp.sin(prop_phase)])
    own_intensity = measured.reshape(PMAX, PATCH, PATCH)
    own_corners = positions.reshape(PMAX, 2)
    own_count = counts.reshape(())
    zero_index = jnp.zeros((), jnp.int32)
    gradient = jnp.zeros(extended.shape, jnp.float32)

    def add_patch(current, intensity, corner):
        starts = (zero_index, zero_index, corner[0] + HALO, corner[1] + HALO)
        window = lax.dynamic_slice(extended, starts, (2, 2, PATCH, PATCH))
        update = patch_grads(window[0], window[1], probe_field, propagator, intensity, tables)
        present = lax.dynamic_slice(current, starts, (2, 2, PATCH, PATCH))
        return lax.dynamic_update_slice(current, present + update, starts)

    def run_slot(index, current):
        intensity = lax.dynamic_index_in_dim(own_intensity, index, 0, keepdims=False)
        corner = lax.dynamic_index_in_dim(own_corners, index, 0, keepdims=False)
        return add_patch(current, intensity, corner)

    gradient = lax.fori_loop(0, own_count, run_slot, gradient)
    planes = gradient.reshape(4, tile_size + 2 * HALO, tile_size + 2 * HALO)
    core_rows = fold_rows(planes, tile_size)
    operand = fold_cols(core_rows, tile_size)
    summed = lax.psum_scatter(operand, "scan", scatter_dimension=1, tiled=True)
    return summed.reshape(2, 2, summed.shape[1], tile_size)


def solution(mesh):
    placed = (
        P(None, None, "row", "col"),
        P(),
        P(),
        P("row", "col", "scan", None, None, None),
        P("row", "col", "scan", None, None),
        P("row", "col", "scan"),
    )
    return jax.shard_map(
        shards,
        mesh=mesh,
        in_specs=placed,
        out_specs=P(None, None, ("row", "scan"), "col"),
        check_vma=False,
    )
```

profile of v0, /device:TPU:1, one launch (start us, length us, event | category | flops | bytes accessed | tf_op | source)
XLA Modules:
  0.0 412.9 jit_solution(1920912317649788854)
XLA Ops:
  6.5 1.3 fusion.86
  7.8 8.3 %collective-permute-start = (f32[2,2,64,512]{3,2,1,0:T(8,128)S(1)}, f32[2,2,64,512]{3,2,1,0:T(8,128)S(1)}, u32[]{:S(2)}, u32[]{:S(2)}) collective-permute-start(f32[2,2,64,512]{3,2,1,0:T(8,128)S(1)} %get-tuple-element.349), channel_id=1, source_target_pairs={{0,64},{64,128},{128,192},{192,256},{256,320},{320,384},{384,448},... | collective-permute-start | bytes 1572872 | tf_op jit(solution)/shard_map/ppermute | solution.py:26
  16.2 1.3 collective-permute-start.1
  17.5 5.2 %copy.66 = f32[2,2,512,512]{2,3,1,0:T(8,128)} copy(f32[2,2,512,512]{3,2,1,0:T(8,128)} %param.16) | data formatting | bytes 8388608 | tf_op args[0]
  22.7 1.0 fusion.82
  23.7 6.7 %collective-permute-done = f32[2,2,64,512]{3,2,1,0:T(8,128)S(1)} collective-permute-done((f32[2,2,64,512]{3,2,1,0:T(8,128)S(1)}, f32[2,2,64,512]{3,2,1,0:T(8,128)S(1)}, u32[]{:S(2)}, u32[]{:S(2)}) %collective-permute-start) | collective-permute-done | bytes 524320 | tf_op jit(solution)/shard_map/ppermute | solution.py:26
  30.4 0.3 copy.65
  30.7 20.1 %collective-permute-done.1 = f32[2,2,64,512]{3,2,1,0:T(8,128)S(1)} collective-permute-done((f32[2,2,64,512]{3,2,1,0:T(8,128)S(1)}, f32[2,2,64,512]{3,2,1,0:T(8,128)S(1)}, u32[]{:S(2)}, u32[]{:S(2)}) %collective-permute-start.1) | collective-permute-done | bytes 524320 | tf_op jit(solution)/shard_map/ppermute | solution.py:27
  50.8 0.3 copy.67
  51.2 2.8 pad_maximum_fusion.3
  53.9 15.7 %collective-permute-start.2 = (f32[2,2,640,64]{2,3,1,0:T(8,128)}, f32[2,2,640,64]{2,3,1,0:T(8,128)}, u32[]{:S(2)}, u32[]{:S(2)}) collective-permute-start(f32[2,2,640,64]{2,3,1,0:T(8,128)} %get-tuple-element.345), channel_id=1, source_target_pairs={{0,8},{8,16},{16,24},{24,32},{32,40},{40,48},{48,56},{1,9},{9,17},... | collective-permute-start | bytes 1966088 | tf_op jit(solution)/shard_map/ppermute | solution.py:26
  69.6 1.9 collective-permute-start.3
  71.6 1.0 multiply_convert_fusion.1
  72.5 1.0 negate_convert_fusion
  73.8 2.0 copy.69
  75.9 2.5 fusion.87
  78.4 3.4 collective-permute-done.3
  81.9 5.9 %pad_maximum_fusion = f32[2,2,640,640]{2,3,1,0:T(8,128)} fusion(f32[2,2,640,64]{2,3,1,0:T(8,128)} %collective-permute-done.3, f32[2,2,64,512]{2,3,1,0:T(8,128)S(1)} %copy.67, f32[2,2,512,512]{2,3,1,0:T(8,128)} %copy.66, f32[2,2,64,512]{2,3,1,0:T(8,128)S(1)} %copy.65, f32[2,2,640,64]{2,3,1,0:T(8,128)} %collective-permute-done.2), kind=kLoop, calls=%fused_computation.90 | loop fusion | flops 6553600 | bytes 13107200 | tf_op jit(solution)/shard_map/concatenate | solution.py:28
  87.8 3.2 broadcast_in_dim.3.clone
  91.0 33.5 %while.18 = (s32[]{:T(128)}, f32[2,2,640,640]{3,2,1,0:T(8,128)}, s32[]{:T(128)}, s32[3,2]{1,0:T(4,128)S(1)}, f32[2,256,256]{1,2,0:T(8,128)}, /*index=5*/f32[256,...) while((s32[]{:T(128)}, f32[2,2,640,640]{3,2,1,0:T(8,128)}, ...), condition=%wide.region_1.2_spmd, body=%wide.region_0.1_spmd.sunk | while | flops 1618739200 | bytes 35389824 | solution.py:137
  91.8 0.6 fusion.136
  94.6 1.5 subtract_convert_fusion.5
  96.1 0.6 convolution_bitcast_fusion.18
  96.8 1.0 fusion.137
  97.8 0.6 convolution_bitcast_fusion.19
  98.4 1.3 subtract_convert_fusion.6
  99.8 0.6 convolution_bitcast_fusion.20
  100.4 1.0 fusion.138
  101.5 0.6 convolution_bitcast_fusion.21
  102.1 1.4 add_convert_fusion.4
  103.5 0.6 convolution_bitcast_fusion.22
  104.1 1.0 fusion.139
  105.1 0.6 convolution_bitcast_fusion.23
  105.8 1.1 multiply_add_fusion.3
  106.9 1.0 maximum_bitcast_fusion.13
  107.9 1.8 constant_dynamic-slice_fusion.6
  109.7 0.3 copy.117
  110.0 1.3 maximum_add_fusion.2
  111.4 0.3 copy.118
  111.7 12.1 %dynamic_update_slice.9 = f32[2,2,640,640]{3,2,1,0:T(8,128)} dynamic-update-slice(f32[2,2,640,640]{3,2,1,0:T(8,128)} %get-tuple-element.483, f32[2,2,256,256]{3,2,1,0:T(8,128)S(1)} %copy.118, s32[]{:T(128)} %constant.170.clone.1..sunk, s32[]{:T(128)} %constant.170.clone.1..sunk, s32[]{:T(128)S(6)} %select_n.83, s32[]{:T(128)S(6)} %select_n.84) | dynamic-update-slice | bytes 2097156 | tf_op jit(solution)/shard_map/while/body/dynamic_update_slice | solution.py:130
  124.5 1.4 fusion.84
  125.8 6.9 %collective-permute-start.4 = (f32[4,64,640]{2,1,0:T(8,128)S(1)}, f32[4,64,640]{2,1,0:T(8,128)S(1)}, u32[]{:S(2)}, u32[]{:S(2)}) collective-permute-start(f32[4,64,640]{2,1,0:T(8,128)S(1)} %get-tuple-element.344), channel_id=1, source_target_pairs={{0,64},{64,128},{128,192},{192,256},{256,320},{320,384},{384,448},... | collective-permute-start | bytes 1966088 | tf_op jit(solution)/shard_map/ppermute | solution.py:16
  132.7 1.3 collective-permute-start.5
  134.0 2.8 slice.362
  136.8 3.3 collective-permute-done.4
  140.2 1.2 fusion.71
  141.4 7.6 %collective-permute-done.5 = f32[4,64,640]{2,1,0:T(8,128)S(1)} collective-permute-done((f32[4,64,640]{2,1,0:T(8,128)S(1)}, f32[4,64,640]{2,1,0:T(8,128)S(1)}, u32[]{:S(2)}, u32[]{:S(2)}) %collective-permute-start.5) | collective-permute-done | bytes 655392 | tf_op jit(solution)/shard_map/ppermute | solution.py:16
  149.1 2.3 copy-done
  151.4 0.3 fusion.85
  151.8 1.1 copy.72
  152.9 109.4 %collective-permute-start.6 = (f32[4,512,64]{1,2,0:T(8,128)}, f32[4,512,64]{1,2,0:T(8,128)}, u32[]{:S(2)}, u32[]{:S(2)}) collective-permute-start(f32[4,512,64]{1,2,0:T(8,128)} %copy.72), channel_id=1, source_target_pairs={{0,8},{8,16},{16,24},{24,32},{32,40},{40,48},{48,56},{1,9},{9,17},... | collective-permute-start | bytes 1572872 | tf_op jit(solution)/shard_map/ppermute | solution.py:16
  262.6 2.1 collective-permute-start.7
  264.8 5.7 %slice.367 = f32[4,512,512]{2,1,0:T(8,128)} slice(f32[4,512,640]{2,1,0:T(8,128)} %copy-done), slice={[0:4], [0:512], [64:576]} | slice | bytes 8388608 | tf_op jit(solution)/shard_map/slice | solution.py:109
  270.5 1.4 copy.73
  271.8 1.6 slice_add_fusion.1
  273.4 5.8 %scatter-add.16 = f32[4,512,512]{2,1,0:T(8,128)} dynamic-update-slice(f32[4,512,512]{2,1,0:T(8,128)} %slice.367, f32[4,512,64]{2,1,0:T(8,128)S(1)} %slice_add_fusion.1, s32[]{:T(128)} %constant.170.clone.1, s32[]{:T(128)} %constant.170.clone.1, s32[]{:T(128)} %constant.170.clone.1) | dynamic-update-slice | bytes 1048580 | tf_op jit(solution)/shard_map/scatter-add | solution.py:110
  279.2 0.3 copy.75
  279.5 1.6 slice_add_fusion
  281.1 5.8 %scatter-add.19 = f32[4,512,512]{2,1,0:T(8,128)} dynamic-update-slice(f32[4,512,512]{2,1,0:T(8,128)} %scatter-add.16, f32[4,512,64]{2,1,0:T(8,128)S(1)} %slice_add_fusion, s32[]{:T(128)} %constant.170.clone.1, s32[]{:T(128)} %constant.170.clone.1, s32[]{:T(128)} %constant.176.clone.1) | dynamic-update-slice | bytes 1048580 | tf_op jit(solution)/shard_map/scatter-add | solution.py:111
  286.9 6.8 %copy.76 = f32[4,512,512]{2,0,1:T(4,128)} copy(f32[4,512,512]{2,1,0:T(8,128)} %scatter-add.19) | data formatting | bytes 8388608 | tf_op jit(solution)/shard_map/scatter-add | solution.py:111
  293.8 1.3 dynamic-slice.32
  295.7 108.4 %all-reduce.3.cloned.1.call-done = f32[4,512,512]{2,0,1:T(4,128)} async-done(((f32[4,512,512]{2,0,1:T(4,128)}), f32[4,512,512]{2,0,1:T(4,128)}) %all-reduce.3.cloned.1.call-update) | async-done | bytes 4194320
  404.1 1.1 constant_dynamic-slice_fusion.2
  405.1 1.0 copy.111
  (15 shorter events, 0.8 us)
Async XLA Ops:
  6.5 397.5 %all-reduce.3.cloned.1.call-start = ((), (), s32[]{:S(2)}) async-start(), calls=%async_computation | async-start | bytes 8388608
  7.8 22.5 %collective-permute-start = (f32[2,2,64,512]{3,2,1,0:T(8,128)S(1)}, f32[2,2,64,512]{3,2,1,0:T(8,128)S(1)}, u32[]{:S(2)}, u32[]{:S(2)}) collective-permute-start(f32[2,2,64,512]{3,2,1,0:T(8,128)S(1)} %get-tuple-element.349), channel_id=1, source_target_pairs={{0,64},{64,128},{128,192},{192,256},{256,320},{320,384},{384,448},... | collective-permute-start | bytes 1572872 | tf_op jit(solution)/shard_map/ppermute | solution.py:26
  16.2 34.7 %collective-permute-start.1 = (f32[2,2,64,512]{3,2,1,0:T(8,128)S(1)}, f32[2,2,64,512]{3,2,1,0:T(8,128)S(1)}, u32[]{:S(2)}, u32[]{:S(2)}) collective-permute-start(f32[2,2,64,512]{3,2,1,0:T(8,128)S(1)} %get-tuple-element.350), channel_id=1, source_target_pairs={{64,0},{128,64},{192,128},{256,192},{320,256},{384,320},{448,384},... | collective-permute-start | bytes 1572872 | tf_op jit(solution)/shard_map/ppermute | solution.py:27
  51.2 24.6 %copy-start.1 = (s32[1,1,1,3,2]{3,4,2,1,0:T(2,128)S(1)}, s32[1,1,1,3,2]{3,4,2,1,0:T(2,128)}, u32[]{:S(2)}) copy-start(s32[1,1,1,3,2]{3,4,2,1,0:T(2,128)} %param.20) | copy-start | bytes 76
  53.9 24.5 %collective-permute-start.2 = (f32[2,2,640,64]{2,3,1,0:T(8,128)}, f32[2,2,640,64]{2,3,1,0:T(8,128)}, u32[]{:S(2)}, u32[]{:S(2)}) collective-permute-start(f32[2,2,640,64]{2,3,1,0:T(8,128)} %get-tuple-element.345), channel_id=1, source_target_pairs={{0,8},{8,16},{16,24},{24,32},{32,40},{40,48},{48,56},{1,9},{9,17},... | collective-permute-start | bytes 1966088 | tf_op jit(solution)/shard_map/ppermute | solution.py:26
  69.6 12.2 %collective-permute-start.3 = (f32[2,2,640,64]{2,3,1,0:T(8,128)}, f32[2,2,640,64]{2,3,1,0:T(8,128)}, u32[]{:S(2)}, u32[]{:S(2)}) collective-permute-start(f32[2,2,640,64]{2,3,1,0:T(8,128)} %get-tuple-element.346), channel_id=1, source_target_pairs={{8,0},{16,8},{24,16},{32,24},{40,32},{48,40},{56,48},{9,1},{17,9},... | collective-permute-start | bytes 1966088 | tf_op jit(solution)/shard_map/ppermute | solution.py:27
  125.8 14.3 %collective-permute-start.4 = (f32[4,64,640]{2,1,0:T(8,128)S(1)}, f32[4,64,640]{2,1,0:T(8,128)S(1)}, u32[]{:S(2)}, u32[]{:S(2)}) collective-permute-start(f32[4,64,640]{2,1,0:T(8,128)S(1)} %get-tuple-element.344), channel_id=1, source_target_pairs={{0,64},{64,128},{128,192},{192,256},{256,320},{320,384},{384,448},... | collective-permute-start | bytes 1966088 | tf_op jit(solution)/shard_map/ppermute | solution.py:16
  132.7 16.3 %collective-permute-start.5 = (f32[4,64,640]{2,1,0:T(8,128)S(1)}, f32[4,64,640]{2,1,0:T(8,128)S(1)}, u32[]{:S(2)}, u32[]{:S(2)}) collective-permute-start(f32[4,64,640]{2,1,0:T(8,128)S(1)} %get-tuple-element.343), channel_id=1, source_target_pairs={{64,0},{128,64},{192,128},{256,192},{320,256},{384,320},{448,384},... | collective-permute-start | bytes 1966088 | tf_op jit(solution)/shard_map/ppermute | solution.py:16
  149.1 2.3 copy-start
  152.9 117.6 %collective-permute-start.6 = (f32[4,512,64]{1,2,0:T(8,128)}, f32[4,512,64]{1,2,0:T(8,128)}, u32[]{:S(2)}, u32[]{:S(2)}) collective-permute-start(f32[4,512,64]{1,2,0:T(8,128)} %copy.72), channel_id=1, source_target_pairs={{0,8},{8,16},{16,24},{24,32},{32,40},{40,48},{48,56},{1,9},{9,17},... | collective-permute-start | bytes 1572872 | tf_op jit(solution)/shard_map/ppermute | solution.py:16
  262.6 16.5 %collective-permute-start.7 = (f32[4,512,64]{1,2,0:T(8,128)S(1)}, f32[4,512,64]{1,2,0:T(8,128)S(1)}, u32[]{:S(2)}, u32[]{:S(2)}) collective-permute-start(f32[4,512,64]{1,2,0:T(8,128)S(1)} %copy.74), channel_id=1, source_target_pairs={{8,0},{16,8},{24,16},{32,24},{40,32},{48,40},{56,48},{9,1},{17,9},... | collective-permute-start | bytes 1572872 | tf_op jit(solution)/shard_map/ppermute | solution.py:16
Sparse Core Ops, SparseCore 0:
  293.9 110.1 all-reduce.2
where the time goes:
time: 415 us; the launch traced here: 413 us
  waiting for transfers between devices  150 us (36%)
  starting transfers between devices  147 us (35%)
  local copies, waits for them, and re-layouts  67.6 us (16%)
  other arithmetic  27 us (7%)
  between operations  14.3 us (3%)
    ppermute x4, starting transfers between devices, from_behind(): return lax.ppermute(block, axis, route)  120 us
    unnamed x2, waiting for transfers between devices  108 us
    ppermute x2, starting transfers between devices, extended_2(): before = lax.ppermute(last, axis, up)  24 us
    ppermute x2, waiting for transfers between devices, extended_2(): after = lax.ppermute(first, axis, down)  23.6 us
    scatter-add x2, local copies, waits for them, and re-layouts, fold_cols(): return core_cols.at[:, :, tile_size - HALO:].add(pass_cols(left_rim, -1))  12.6 us
    dynamic_update_slice x2, local copies, waits for them, and re-layouts, add_patch(): return lax.dynamic_update_slice(current, present + update, starts)  12.4 us
    ppermute x4, waiting for transfers between devices, from_behind(): return lax.ppermute(block, axis, route)  10.9 us
    unnamed x7, local copies, waits for them, and re-layouts  9.94 us
  transfers between devices with their start and end apart: 9, of which 6 were waited for; matrix products, arithmetic and copies ran while one was open for 8% of the time, Pallas kernels for 0%

commit v1 on v0

v1 whole, which is shorter than its diff:
```python
import functools
import math

import jax
import jax.numpy as jnp
import numpy as np
from jax import lax
from jax.experimental import pallas as pl
from jax.experimental.pallas import tpu as pltpu
from jax.sharding import PartitionSpec as P

PATCH = 256
HALO = 64
PMAX = 3
LANE = 128
BLOCK = 64
PIECE = 8
FAR = 4
CHAINS = ((1, 0, 3), (1, 1, 4), (-1, 0, 4), (-1, 1, 3))
MESH = pl.DeviceIdType.MESH


def halo_kernel(sizes, field_ref, phase_ref, probe_ref, half_ref, measured_ref, ext_ref, prop_ref, probe_out, measured_out,
                fwd_ref, inv_ref, halves, load_sem, core_sem, row_send, row_recv, ring_send, ring_recv,
                side_send, side_recv, corner_send, corner_recv):
    rows, cols, depth = sizes
    r, c, z = (lax.axis_index(name) for name in ("row", "col", "scan"))
    has_left, has_right = c > 0, c < cols - 1
    has_up, has_down = r > 0, r < rows - 1
    around = lambda step: lax.rem(z + (step + depth), depth)
    core = field_ref.shape[1]
    barrier = pltpu.get_barrier_semaphore()

    def greet(device):
        pl.semaphore_signal(barrier, inc=1, device_id=device, device_id_type=MESH)

    for step in (1, -1):
        greet((r, c, around(step)))
    pl.when(has_left)(lambda: greet((r, c - 1, z)))
    pl.when(has_right)(lambda: greet((r, c + 1, z)))
    pl.when(has_up)(lambda: greet((r - 1, c, z)))
    pl.when(has_down)(lambda: greet((r + 1, c, z)))

    fills = [
        pltpu.make_async_copy(
            field_ref.at[:, :, t * LANE : (t + 1) * LANE], ext_ref.at[:, t + 1, HALO : HALO + core, :], core_sem.at[t])
        for t in range(4)
    ]
    for fill in fills:
        fill.start()
    loads = [
        pltpu.make_async_copy(source, target, load_sem.at[i])
        for i, (source, target) in enumerate((
            (phase_ref, prop_ref.at[0]), (half_ref, halves), (probe_ref, probe_out), (measured_ref, measured_out)))
    ]
    for load in loads:
        load.start()
    for fill in fills:
        fill.wait()

    count = jnp.int32(2)
    for flag in (has_left, has_right, has_up, has_down):
        count = count + flag.astype(jnp.int32)
    pl.semaphore_wait(barrier, count)

    def piece_rows(first, piece):
        return pl.ds(pl.multiple_of(first + piece * PIECE, PIECE), PIECE)

    starts = (0, HALO + core)

    def row_copy(side):
        source = piece_rows(core if side == 0 else HALO, z)
        return pltpu.make_async_remote_copy(
            src_ref=ext_ref.at[:, 1:5, source, :], dst_ref=ext_ref.at[:, 1:5, piece_rows(starts[side], z), :],
            send_sem=row_send.at[side], recv_sem=row_recv.at[side],
            device_id=(r + 1 - 2 * side, c, z), device_id_type=MESH)

    pl.when(has_down)(lambda: row_copy(0).start())
    pl.when(has_up)(lambda: row_copy(1).start())

    def side_copy(side):
        tile, target = ((4, 0), (1, 5))[side]
        return pltpu.make_async_remote_copy(
            src_ref=ext_ref.at[:, tile, HALO : HALO + core, :], dst_ref=ext_ref.at[:, target, HALO : HALO + core, :],
            send_sem=side_send.at[side], recv_sem=side_recv.at[side],
            device_id=(r, c + 1 - 2 * side, z), device_id_type=MESH)

    pl.when(has_right)(lambda: side_copy(0).start())
    pl.when(has_left)(lambda: side_copy(1).start())

    def ring_copy(side, chain, step):
        direction, part, _ = CHAINS[chain]
        place = ext_ref.at[:, 2 * part + 1 : 2 * part + 3, piece_rows(starts[side], around(-direction * step)), :]
        return pltpu.make_async_remote_copy(
            src_ref=place, dst_ref=place,
            send_sem=ring_send.at[side, chain, step], recv_sem=ring_recv.at[side, chain, step],
            device_id=(r, c, around(direction)), device_id_type=MESH)

    def corner_copy(side, part, piece, slot):
        tile, target = ((1, 5), (4, 0))[part]
        place = piece_rows(starts[side], piece)
        return pltpu.make_async_remote_copy(
            src_ref=ext_ref.at[:, tile, place, :], dst_ref=ext_ref.at[:, target, place, :],
            send_sem=corner_send.at[side, part, slot], recv_sem=corner_recv.at[side, part, slot],
            device_id=(r, c + 2 * part - 1, z), device_id_type=MESH)

    faces = ((has_left, has_right), (has_right, has_left))
    live = (has_up, has_down)
    corners = []

    def send_corner(side, part, offset):
        slot = len([1 for entry in corners if entry[:2] == (side, part)])
        corners.append((side, part, offset, slot))
        pl.when(faces[part][0])(lambda: corner_copy(side, part, around(offset), slot).start())

    loads[0].wait()
    phase = prop_ref[0]
    prop_ref[0] = jnp.cos(phase)
    prop_ref[1] = jnp.sin(phase)
    loads[1].wait()
    cosines, sines = halves[0], halves[1]
    for ref, above, below in ((fwd_ref, sines, -sines), (inv_ref, -sines, sines)):
        ref[:PATCH, :PATCH] = cosines
        ref[PATCH:, PATCH:] = cosines
        ref[:PATCH, PATCH:] = above
        ref[PATCH:, :PATCH] = below

    for step in range(FAR + 1):
        for side in range(2):
            @pl.when(live[side])
            def _():
                if step == 0:
                    row_copy(side).wait_recv()
                    for part in range(2):
                        send_corner(side, part, 0)
                for chain, (direction, part, length) in enumerate(CHAINS):
                    if 0 < step <= length:
                        ring_copy(side, chain, step - 1).wait_recv()
                    if step < length:
                        ring_copy(side, chain, step).start()
                    if 0 < step <= length:
                        send_corner(side, part, -direction * step)

    for side in range(2):
        pl.when((has_left, has_right)[side])(lambda: side_copy(side).wait_recv())
        @pl.when(live[side])
        def _():
            for entry_side, part, offset, slot in corners:
                if entry_side == side:
                    pl.when(faces[part][1])(lambda: corner_copy(side, part, around(offset), slot).wait_recv())
                    pl.when(faces[part][0])(lambda: corner_copy(side, part, around(offset), slot).wait_send())
            for chain, (_, _, length) in enumerate(CHAINS):
                for step in range(length):
                    ring_copy(side, chain, step).wait_send()
    for load in loads[2:]:
        load.wait()
    pl.when(has_down)(lambda: row_copy(0).wait_send())
    pl.when(has_up)(lambda: row_copy(1).wait_send())
    pl.when(has_right)(lambda: side_copy(0).wait_send())
    pl.when(has_left)(lambda: side_copy(1).wait_send())

def halo_call(sizes, field, phase, probe, halves, measured):
    planes, core, _ = field.shape
    dma = pltpu.SemaphoreType.DMA
    depth = sizes[2]
    vmem = pl.BlockSpec(memory_space=pltpu.VMEM)
    return pl.pallas_call(
        functools.partial(halo_kernel, sizes),
        out_shape=(
            jax.ShapeDtypeStruct((planes, 6, core + 2 * HALO, LANE), jnp.float32),
            jax.ShapeDtypeStruct((2, PATCH, PATCH), jnp.float32),
            jax.ShapeDtypeStruct(probe.shape, jnp.float32),
            jax.ShapeDtypeStruct(measured.shape, jnp.float32),
            jax.ShapeDtypeStruct((2 * PATCH, 2 * PATCH), jnp.bfloat16),
            jax.ShapeDtypeStruct((2 * PATCH, 2 * PATCH), jnp.bfloat16),
        ),
        in_specs=[pl.BlockSpec(memory_space=pltpu.HBM)] * 5,
        out_specs=(vmem,) * 6,
        scratch_shapes=[
            pltpu.VMEM((2, PATCH, PATCH), jnp.bfloat16), dma((4,)),
            dma((4,)), dma((2,)), dma((2,)), dma((2, 4, FAR)), dma((2, 4, FAR)),
            dma((2,)), dma((2,)), dma((2, 2, depth)), dma((2, 2, depth)),
        ],
        compiler_params=pltpu.CompilerParams(collective_id=0, has_side_effects=True, vmem_limit_bytes=24 << 20),
    )(field, phase, probe, halves, measured)


def dft_halves():
    k = np.arange(PATCH)
    ang = ((k[:,None]*k[None,:])%PATCH).astype(np.float32)*np.float32(2.0*math.pi/PATCH)
    scale = np.float32(math.sqrt(PATCH))
    return np.stack([np.cos(ang)/scale, np.sin(ang)/scale]).astype(jnp.bfloat16)

def transform(real, imag, left, right):
    rows = jnp.concatenate([real, imag], 0)
    middle = jnp.dot(left, rows, preferred_element_type=jnp.float32).astype(jnp.bfloat16)
    middle = jnp.concatenate([middle[:PATCH], middle[PATCH:]], 1)
    out = jnp.dot(middle, right, preferred_element_type=jnp.float32)
    return out[:, :PATCH], out[:, PATCH:]

def patch_kernel(count_ref, corner_ref, object_ref, prop_ref, probe_ref, measured_ref, fwd_ref, inv_ref, grad_ref):
    grad_ref[...] = jnp.zeros_like(grad_ref)
    bf = lambda x: x.astype(jnp.bfloat16)

    def slot(k, carry):
        row = corner_ref[0, k] + HALO
        col = corner_ref[1, k] + LANE
        tile = col // LANE
        shift = col - tile * LANE
        back = lax.rem(LANE - shift, LANE)
        lanes = lax.broadcasted_iota(jnp.int32, (PATCH, LANE), 1)
        early, late = lanes < LANE - shift, lanes < shift
        def window(plane):
            turned = [pltpu.roll(object_ref[plane, tile + t, pl.ds(row, PATCH), :], back, 1) for t in range(3)]
            return jnp.concatenate([jnp.where(early, turned[0], turned[1]), jnp.where(early, turned[1], turned[2])], 1)
        def place(plane, value):
            first, second = (pltpu.roll(value[:, t*LANE:(t+1)*LANE], shift, 1) for t in range(2))
            zero = jnp.zeros_like(first)
            for t, part in enumerate((jnp.where(late, zero, first), jnp.where(late, first, second), jnp.where(late, second, zero))):
                grad_ref[plane, tile + t, pl.ds(row, PATCH), :] += part
        pr, pi = probe_ref[0], probe_ref[1]
        hr, hi = prop_ref[0], prop_ref[1]
        fwd, inv = fwd_ref, inv_ref
        ar, ai = window(0), window(1)
        sr, si = transform(bf(pr*ar-pi*ai), bf(pr*ai+pi*ar), fwd[...], inv[...])
        wr, wi = transform(bf(hr*sr-hi*si), bf(hr*si+hi*sr), inv[...], fwd[...])
        br, bi = window(2), window(3)
        fr, fi = transform(bf(br*wr-bi*wi), bf(br*wi+bi*wr), fwd[...], inv[...])
        level = fr*fr + fi*fi - measured_ref[k]
        gr, gi = transform(bf(level*fr), bf(level*fi), inv[...], fwd[...])
        place(2, wr*gr+wi*gi)
        place(3, wr*gi-wi*gr)
        tr, ti = transform(bf(br*gr+bi*gi), bf(br*gi-bi*gr), fwd[...], inv[...])
        qr, qi = transform(bf(hr*tr+hi*ti), bf(hr*ti-hi*tr), inv[...], fwd[...])
        place(0, pr*qr+pi*qi)
        place(1, pr*qi-pi*qr)
        return carry
    lax.fori_loop(0, count_ref[0], slot, 0)

def patch_call(count, corners, ext, *rest):
    v = pl.BlockSpec(memory_space=pltpu.VMEM); s = pl.BlockSpec(memory_space=pltpu.SMEM)
    return pl.pallas_call(patch_kernel,
        out_shape=jax.ShapeDtypeStruct(ext.shape, jnp.float32),
        in_specs=[s, s] + [v] * 6, out_specs=v,
        compiler_params=pltpu.CompilerParams(vmem_limit_bytes=24<<20),
    )(count, corners, ext, *rest)


def reduce_kernel(sizes, grad_ref, out_ref, pack, took, stage, rim, rim_slot, slot, rim_sum, far,
                  fold_send, fold_recv, rim_send, rim_recv, main_send, main_recv, far_send, far_recv):
    rows, cols, depth = sizes
    r, c, z = (lax.axis_index(name) for name in ("row", "col", "scan"))
    last = depth - 1
    has_left, has_right = c > 0, c < cols - 1
    has_up, has_down = r > 0, r < rows - 1
    takes_top = jnp.logical_and(z == last, has_down)
    takes_bottom = jnp.logical_and(z == 0, has_up)
    around = lambda step: lax.rem(z + (step + depth), depth)
    barrier = pltpu.get_barrier_semaphore()

    def greet(device):
        pl.semaphore_signal(barrier, inc=1, device_id=device, device_id_type=MESH)

    for step in (1, -1):
        greet((r, c, around(step)))
    pl.when(has_left)(lambda: greet((r, c - 1, z)))
    pl.when(has_right)(lambda: greet((r, c + 1, z)))

    @pl.when(takes_top)
    def _():
        for other in range(depth):
            greet((r + 1, c, other))

    @pl.when(takes_bottom)
    def _():
        for other in range(depth):
            greet((r - 1, c, other))

    blocks = grad_ref.shape[2] // BLOCK
    half = BLOCK // 2
    for side, tile in ((0, 0), (1, 5)):
        for b in range(blocks):
            top = grad_ref[:, tile, b * BLOCK : b * BLOCK + half, :]
            low = grad_ref[:, tile, b * BLOCK + half : (b + 1) * BLOCK, :]
            pack[side, b] = top + pltpu.roll(low, BLOCK, 2)

    count = jnp.int32(2)
    for flag in (has_left, has_right, has_up, has_down):
        count = count + flag.astype(jnp.int32)
    pl.semaphore_wait(barrier, count)

    def fold_copy(side, block):
        return pltpu.make_async_remote_copy(
            src_ref=pack.at[side, block], dst_ref=took.at[side, block],
            send_sem=fold_send.at[side, block], recv_sem=fold_recv.at[side, block],
            device_id=(r, c + (2 * side - 1), z), device_id_type=MESH)

    steps = (4, 3, -3, 2, -2, 1, -1, 0)
    order = [0, blocks - 1] + [around(step) + 1 for step in steps]

    @pl.when(has_left)
    def _():
        for b in order:
            fold_copy(0, b).start()

    @pl.when(has_right)
    def _():
        for b in order:
            fold_copy(1, b).start()

    @pl.when(jnp.logical_not(has_right))
    def _():
        took[0] = jnp.zeros_like(took[0])

    @pl.when(jnp.logical_not(has_left))
    def _():
        took[1] = jnp.zeros_like(took[1])

    def await_fold(block):
        pl.when(has_right)(lambda: fold_copy(0, block).wait_recv())
        pl.when(has_left)(lambda: fold_copy(1, block).wait_recv())

    right_lanes = lax.broadcasted_iota(jnp.int32, (half, LANE), 1) >= BLOCK

    def local(block, plane, part):
        start = pl.multiple_of(block * BLOCK, BLOCK)
        tiles = [grad_ref[plane, 2 * part + 1 + t, pl.ds(start, BLOCK), :] for t in range(2)]
        side, edge = (1, 0) if part == 0 else (0, 1)
        packed = took[side, block, plane]
        turned = pltpu.roll(packed, BLOCK, 1)
        zero = jnp.zeros_like(packed)
        if part == 0:
            pieces = [jnp.where(right_lanes, zero, packed), jnp.where(right_lanes, zero, turned)]
        else:
            pieces = [jnp.where(right_lanes, packed, zero), jnp.where(right_lanes, turned, zero)]
        tiles[edge] = tiles[edge] + jnp.concatenate(pieces, 0)
        return tiles

    for index, block in enumerate((0, blocks - 1)):
        await_fold(block)
        for part in range(2):
            for plane in range(4):
                for t, tile in enumerate(local(block, plane, part)):
                    rim[part, index, plane, t] = tile

    def rim_copy(chain, step, source):
        direction = CHAINS[chain][0]
        return pltpu.make_async_remote_copy(
            src_ref=source, dst_ref=rim_slot.at[chain, step],
            send_sem=rim_send.at[chain, step], recv_sem=rim_recv.at[chain, step],
            device_id=(r, c, around(direction)), device_id_type=MESH)

    def main_copy(chain, step, sub, source):
        direction = CHAINS[chain][0]
        return pltpu.make_async_remote_copy(
            src_ref=source, dst_ref=slot.at[chain, step, sub],
            send_sem=main_send.at[chain, step, sub], recv_sem=main_recv.at[chain, step, sub],
            device_id=(r, c, around(direction)), device_id_type=MESH)

    def rim_rows(piece):
        return pl.ds(pl.multiple_of(piece * PIECE, PIECE), PIECE)

    sent = []

    def rim_round(k):
        for chain, (direction, part, length) in enumerate(CHAINS):
            step = k - (FAR - length)
            if step < 0:
                continue
            piece = rim_rows(around(direction * (FAR - k)))
            if step == 0:
                source = rim.at[part, :, :, :, piece, :]
            else:
                source = rim_slot.at[chain, step - 1]
                rim_copy(chain, step - 1, source).wait_recv()
                source[...] += rim[part, :, :, :, piece, :]
            copy = rim_copy(chain, step, source)
            copy.start()
            sent.append(copy)

    def main_round(k, sub):
        for chain, (direction, part, length) in enumerate(CHAINS):
            step = k - (FAR - length)
            if step < 0:
                continue
            block = around(direction * (FAR - k)) + 1
            if step == 0:
                source = stage.at[chain, sub]
            else:
                source = slot.at[chain, step - 1, sub]
                main_copy(chain, step - 1, sub, source).wait_recv()
            for p in range(2):
                for t, tile in enumerate(local(block, 2 * sub + p, part)):
                    if step == 0:
                        source[p, t] = tile
                    else:
                        source[p, t] += tile
            copy = main_copy(chain, step, sub, source)
            copy.start()
            sent.append(copy)

    def await_round(k):
        for step in ((4,), (3, -3), (2, -2), (1, -1), (0,))[k]:
            await_fold(around(step) + 1)

    rim_round(0)
    await_round(0)
    main_round(0, 0)
    rim_round(1)
    main_round(0, 1)
    rim_round(2)
    await_round(1)
    main_round(1, 0)
    rim_round(3)
    main_round(1, 1)
    own = rim_rows(z)
    for chain, (direction, part, length) in enumerate(CHAINS):
        rim_copy(chain, length - 1, rim_slot.at[chain, length - 1]).wait_recv()
    for part in range(2):
        ahead, behind = [(i, n) for i, (_, q, n) in enumerate(CHAINS) if q == part]
        total = rim[part, :, :, :, own, :] + rim_slot[ahead[0], ahead[1] - 1] + rim_slot[behind[0], behind[1] - 1]
        rim_sum[:, :, 2 * part : 2 * part + 2] = total

    def far_copy(side):
        target = (r - 1, c, last) if side == 0 else (r + 1, c, 0)
        return pltpu.make_async_remote_copy(
            src_ref=rim_sum.at[side], dst_ref=far.at[:, :, own, :],
            send_sem=far_send.at[side], recv_sem=far_recv.at[z],
            device_id=target, device_id_type=MESH)

    pl.when(has_up)(lambda: far_copy(0).start())
    pl.when(has_down)(lambda: far_copy(1).start())
    await_round(2)
    main_round(2, 0)
    main_round(2, 1)
    await_round(3)
    main_round(3, 0)
    main_round(3, 1)
    await_round(4)

    for sub in range(2):
        for chain, (direction, part, length) in enumerate(CHAINS):
            main_copy(chain, length - 1, sub, slot.at[chain, length - 1, sub]).wait_recv()
        for part in range(2):
            ahead, behind = [(i, n) for i, (_, q, n) in enumerate(CHAINS) if q == part]
            for p in range(2):
                tiles = local(z + 1, 2 * sub + p, part)
                for t in range(2):
                    out_ref[2 * sub + p, :, (2 * part + t) * LANE : (2 * part + t + 1) * LANE] = (
                        tiles[t] + slot[ahead[0], ahead[1] - 1, sub, p, t] + slot[behind[0], behind[1] - 1, sub, p, t])

    @pl.when(jnp.logical_or(takes_top, takes_bottom))
    def _():
        for other in range(depth):
            pltpu.make_async_remote_copy(
                src_ref=rim_sum.at[0], dst_ref=far.at[:, :, other * PIECE : (other + 1) * PIECE, :],
                send_sem=far_send.at[0], recv_sem=far_recv.at[other],
                device_id=(r, c, around(1)), device_id_type=MESH).wait_recv()
        for plane in range(4):
            for t in range(4):
                out_ref[plane, :, t * LANE : (t + 1) * LANE] += far[plane, t]

    for copy in sent:
        copy.wait_send()
    pl.when(has_up)(lambda: far_copy(0).wait_send())
    pl.when(has_down)(lambda: far_copy(1).wait_send())

    @pl.when(has_left)
    def _():
        for b in range(blocks):
            fold_copy(0, b).wait_send()

    @pl.when(has_right)
    def _():
        for b in range(blocks):
            fold_copy(1, b).wait_send()

def reduce_call(sizes, grad):
    blocks = grad.shape[2] // BLOCK
    f32 = jnp.float32
    dma = pltpu.SemaphoreType.DMA
    return pl.pallas_call(
        functools.partial(reduce_kernel, sizes),
        out_shape=jax.ShapeDtypeStruct((4, BLOCK, 4 * LANE), f32),
        in_specs=[pl.BlockSpec(memory_space=pltpu.VMEM)],
        out_specs=pl.BlockSpec(memory_space=pltpu.VMEM),
        scratch_shapes=[
            pltpu.VMEM((2, blocks, 4, BLOCK // 2, LANE), f32),
            pltpu.VMEM((2, blocks, 4, BLOCK // 2, LANE), f32),
            pltpu.VMEM((4, 2, 2, 2, BLOCK, LANE), f32),
            pltpu.VMEM((2, 2, 4, 2, BLOCK, LANE), f32),
            pltpu.VMEM((4, FAR, 2, 4, 2, PIECE, LANE), f32),
            pltpu.VMEM((4, FAR, 2, 2, 2, BLOCK, LANE), f32),
            pltpu.VMEM((2, 4, 4, PIECE, LANE), f32),
            pltpu.VMEM((4, 4, BLOCK, LANE), f32),
            dma((2, blocks)), dma((2, blocks)),
            dma((4, FAR)), dma((4, FAR)),
            dma((4, FAR, 2)), dma((4, FAR, 2)),
            dma((2,)), dma((sizes[2],)),
        ],
        compiler_params=pltpu.CompilerParams(collective_id=1, has_side_effects=True, vmem_limit_bytes=32 << 20),
    )(grad)


def shards(sizes, object_field, probe_field, prop_phase, measured, positions, counts):
    loaded = halo_call(
        sizes,
        object_field.reshape(4, *object_field.shape[2:]),
        prop_phase,
        probe_field,
        jnp.asarray(dft_halves()),
        measured.reshape(PMAX, PATCH, PATCH),
    )
    gradient = patch_call(counts.reshape(1), positions.reshape(PMAX, 2).T, *loaded)
    return reduce_call(sizes, gradient).reshape(2, 2, BLOCK, 4 * LANE)


def solution(mesh):
    placed = (
        P(None, None, "row", "col"),
        P(),
        P(),
        P("row", "col", "scan", None, None, None),
        P("row", "col", "scan", None, None),
        P("row", "col", "scan"),
    )
    sizes = tuple(mesh.shape[name] for name in ("row", "col", "scan"))
    return jax.shard_map(
        functools.partial(shards, sizes),
        mesh=mesh,
        in_specs=placed,
        out_specs=P(None, None, ("row", "scan"), "col"),
        check_vma=False,
    )
```

time: 415 us -> 133 us (0.32)
  the two profiles are of different devices: /device:TPU:1 before, /device:TPU:10 now
where the time goes in v1:
time: 133 us; the launch traced here: 131 us
  Pallas kernels  123 us (92%)
  local copies, waits for them, and re-layouts  7.72 us (6%)
    pallas_call x1, Pallas kernels, reduce_call(): pl.pallas_call(functools.partial(reduce_kernel, sizes), out_shape=jax.Sha...  71.2 us
    pallas_call x1, Pallas kernels, halo_call(): pl.pallas_call(functools.partial(halo_kernel, sizes), out_shape=(jax.Shap...  37.5 us
    pallas_call x1, Pallas kernels, patch_call(): pl.pallas_call(patch_kernel, out_shape=jax.ShapeDtypeStruct(ext.shape, jn...  14.1 us
    unnamed x13, local copies, waits for them, and re-layouts  7.72 us

profile of v1, /device:TPU:10, one launch (start us, length us, event | category | flops | bytes accessed | tf_op | source)
XLA Modules:
  0.0 131.3 jit_solution(16098465843392180424)
XLA Ops:
  0.7 0.0 copy-start
  0.7 2.2 %copy-done = f32[2,2,512,512]{3,2,1,0:T(8,128)S(1)} copy-done((f32[2,2,512,512]{3,2,1,0:T(8,128)S(1)}, f32[2,2,512,512]{3,2,1,0:T(8,128)}, u32[]{:S(2)}) %copy-start) | copy-done | bytes 4194328
  2.8 0.0 copy-start.1
  2.8 1.1 copy-done.1
  4.0 0.0 copy-start.2
  4.0 1.0 copy-done.2
  5.0 0.0 copy-start.3
  5.0 0.9 copy-done.3
  6.0 0.0 copy-start.4
  6.0 0.9 copy-done.4
  6.9 37.5 %shard_map.73 = (f32[4,6,640,128]{3,2,1,0:T(8,128)S(1)}, f32[2,256,256]{2,1,0:T(8,128)S(1)}, f32[2,256,256]{2,1,0:T(8,128)S(1)}, f32[3,256,256]{2,1,0:T(8,128)S(...) custom-call(f32[4,512,512]{2,1,0:T(8,128)S(1)} %bitcast.8, f32[256,256]{1,0:T(8,128)S(1)} %copy-done.3, ...), custom_call_target="tpu_custom_call" | custom-call | tf_op jit(solution)/shard_map/pallas_call | solution.py:167
  44.4 0.0 copy-start.5
  44.5 0.7 copy-done.5
  45.1 14.1 %shard_map.74.grad_ref = f32[4,6,640,128]{3,2,1,0:T(8,128)S(1)} custom-call(s32[1]{0:T(128)} %bitcast.7.count_ref, s32[2,3]{1,0:T(2,128)S(1)} %bitcast.11, f32[4,6,640,128]{3,2,1,0:T(8,128)S(1)} %get-tuple-element.11.object_ref, f32[2,256,256]{2,1,0:T(8,128)S(1)} %get-tuple-element.12.prop_ref, f32[2,256,256]{2,1,0:T(8,128)S(1)} %get-tuple-element.13.probe_ref, ...), custom_call_target="tpu_custom_call" | custom-call | tf_op jit(solution)/shard_map/pallas_call | solution.py:242
  59.2 71.2 %shard_map.75 = f32[4,64,512]{2,1,0:T(8,128)S(1)} custom-call(f32[4,6,640,128]{3,2,1,0:T(8,128)S(1)} %shard_map.74.grad_ref), custom_call_target="tpu_custom_call" | custom-call | tf_op jit(solution)/shard_map/pallas_call | solution.py:482
  130.5 0.8 copy.10
Async XLA Ops:
  0.7 2.2 %copy-start = (f32[2,2,512,512]{3,2,1,0:T(8,128)S(1)}, f32[2,2,512,512]{3,2,1,0:T(8,128)}, u32[]{:S(2)}) copy-start(f32[2,2,512,512]{3,2,1,0:T(8,128)} %param.7) | copy-start | bytes 12582916
  2.8 1.1 copy-start.1
  4.0 1.0 copy-start.2
  5.0 0.9 copy-start.3
  6.0 0.9 copy-start.4
  44.4 0.7 copy-start.5

commit v2 on v0

v2 whole, which is shorter than its diff:
```python
import functools
import math

import jax
import jax.numpy as jnp
import numpy as np
from jax import lax
from jax.experimental import pallas as pl
from jax.experimental.pallas import tpu as pltpu
from jax.sharding import PartitionSpec as P

PATCH = 256
HALO = 64
PMAX = 3
LANE = 128
BLOCK = 64
PIECE = 8
FAR = 4
CHAINS = ((1, 0, 3), (1, 1, 4), (-1, 0, 4), (-1, 1, 3))
MESH = pl.DeviceIdType.MESH


def dft_halves():
    k = np.arange(PATCH)
    angles = ((k[:, None] * k[None, :]) % PATCH).astype(np.float32) * np.float32(2.0 * math.pi / PATCH)
    scale = np.float32(math.sqrt(PATCH))
    return np.stack([np.cos(angles) / scale, np.sin(angles) / scale]).astype(jnp.bfloat16)


def stacked(real, imag):
    return jnp.concatenate([real.astype(jnp.bfloat16), imag.astype(jnp.bfloat16)], 0)


def transform(rows, left, right):
    middle = jnp.dot(left, rows, preferred_element_type=jnp.float32).astype(jnp.bfloat16)
    middle = jnp.concatenate([middle[:PATCH], middle[PATCH:]], 1)
    out = jnp.dot(middle, right, preferred_element_type=jnp.float32)
    return out[:, :PATCH], out[:, PATCH:]


def fused_kernel(
    sizes, count_ref, corner_ref, field_ref, phase_ref, probe_hbm, half_ref, measured_hbm, out_ref,
    ext_ref, prop_ref, probe_ref, measured_ref, fwd_ref, inv_ref, halves, through, placed,
    pack, took, stage, rim, rim_slot, slot, rim_sum, far,
    load_sem, core_sem, row_send, row_recv, ring_send, ring_recv, side_send, side_recv, corner_send, corner_recv,
    fold_send, fold_recv, rim_send, rim_recv, main_send, main_recv, far_send, far_recv,
):
    rows, cols, depth = sizes
    r, c, z = (lax.axis_index(name) for name in ("row", "col", "scan"))
    last = depth - 1
    has_left, has_right = c > 0, c < cols - 1
    has_up, has_down = r > 0, r < rows - 1
    core = field_ref.shape[1]
    blocks = ext_ref.shape[2] // BLOCK
    half = BLOCK // 2

    def around(step):
        return lax.rem(z + (step + depth), depth)

    def remote(source, target, send, recv, device):
        return pltpu.make_async_remote_copy(
            src_ref=source, dst_ref=target, send_sem=send, recv_sem=recv, device_id=device, device_id_type=MESH
        )

    barrier = pltpu.get_barrier_semaphore()

    def greet(device):
        pl.semaphore_signal(barrier, inc=1, device_id=device, device_id_type=MESH)

    pl.when(has_up)(lambda: greet((r - 1, c, z)))
    pl.when(has_down)(lambda: greet((r + 1, c, z)))
    pl.when(has_left)(lambda: greet((r, c - 1, z)))
    pl.when(has_right)(lambda: greet((r, c + 1, z)))
    for step in (1, -1):
        greet((r, c, around(step)))

    fills = [
        pltpu.make_async_copy(
            field_ref.at[:, :, t * LANE : (t + 1) * LANE], ext_ref.at[:, t + 1, HALO : HALO + core, :], core_sem.at[t]
        )
        for t in range(4)
    ]
    for fill in fills:
        fill.start()
    pairs = ((phase_ref, prop_ref.at[0]), (half_ref, halves), (probe_hbm, probe_ref), (measured_hbm, measured_ref))
    loads = [pltpu.make_async_copy(source, target, load_sem.at[i]) for i, (source, target) in enumerate(pairs)]
    for load in loads:
        load.start()
    for fill in fills:
        fill.wait()
    count = jnp.int32(2)
    for flag in (has_left, has_right, has_up, has_down):
        count = count + flag.astype(jnp.int32)
    pl.semaphore_wait(barrier, count)

    def piece_rows(first, piece):
        return pl.ds(pl.multiple_of(first + piece * PIECE, PIECE), PIECE)

    starts = (0, HALO + core)

    def row_copy(side):
        source = piece_rows(core if side == 0 else HALO, z)
        return remote(
            ext_ref.at[:, 1:5, source, :], ext_ref.at[:, 1:5, piece_rows(starts[side], z), :],
            row_send.at[side], row_recv.at[side], (r + 1 - 2 * side, c, z),
        )

    def side_copy(side):
        tile, target = ((4, 0), (1, 5))[side]
        return remote(
            ext_ref.at[:, tile, HALO : HALO + core, :], ext_ref.at[:, target, HALO : HALO + core, :],
            side_send.at[side], side_recv.at[side], (r, c + 1 - 2 * side, z),
        )

    def ring_copy(side, chain, step):
        direction, part, _ = CHAINS[chain]
        place = ext_ref.at[:, 2 * part + 1 : 2 * part + 3, piece_rows(starts[side], around(-direction * step)), :]
        return remote(
            place, place, ring_send.at[side, chain, step], ring_recv.at[side, chain, step], (r, c, around(direction))
        )

    def corner_copy(side, part, offset, index):
        tile, target = ((1, 5), (4, 0))[part]
        place = piece_rows(starts[side], around(offset))
        return remote(
            ext_ref.at[:, tile, place, :], ext_ref.at[:, target, place, :],
            corner_send.at[side, part, index], corner_recv.at[side, part, index], (r, c + 2 * part - 1, z),
        )

    pl.when(has_down)(lambda: row_copy(0).start())
    pl.when(has_up)(lambda: row_copy(1).start())

    loads[0].wait()
    phase = prop_ref[0]
    prop_ref[0] = jnp.cos(phase)
    prop_ref[1] = jnp.sin(phase)
    loads[1].wait()
    cosines, sines = halves[0], halves[1]
    for ref, above, below in ((fwd_ref, sines, -sines), (inv_ref, -sines, sines)):
        ref[:PATCH, :PATCH] = cosines
        ref[PATCH:, PATCH:] = cosines
        ref[:PATCH, PATCH:] = above
        ref[PATCH:, :PATCH] = below

    targets = ((has_left, has_right), (has_right, has_left))
    live = (has_up, has_down)
    corners = []

    def send_corner(side, part, offset):
        index = len([1 for entry in corners if entry[:2] == (side, part)])
        corners.append((side, part, offset, index))
        pl.when(targets[part][0])(lambda: corner_copy(side, part, offset, index).start())

    for step in range(FAR + 1):
        for side in range(2):

            @pl.when(live[side])
            def _():
                if step == 0:
                    row_copy(side).wait_recv()
                for chain, (direction, part, length) in enumerate(CHAINS):
                    if 0 < step <= length:
                        ring_copy(side, chain, step - 1).wait_recv()
                    if step < length:
                        ring_copy(side, chain, step).start()
                for chain, (direction, part, length) in enumerate(CHAINS):
                    if step == 0 and chain < 2:
                        send_corner(side, chain, 0)
                    if 0 < step <= length:
                        send_corner(side, part, -direction * step)

        if step == 0:
            pl.when(has_right)(lambda: side_copy(0).start())
            pl.when(has_left)(lambda: side_copy(1).start())
            placed[...] = jnp.zeros_like(placed)

    for side in range(2):
        pl.when((has_left, has_right)[side])(lambda: side_copy(side).wait_recv())

        @pl.when(live[side])
        def _():
            for at, part, offset, index in corners:
                if at == side:
                    pl.when(targets[part][1])(lambda: corner_copy(side, part, offset, index).wait_recv())

    for load in loads[2:]:
        load.wait()

    def position(k):
        row = jnp.clip(corner_ref[0, k], -HALO, core + HALO - PATCH) + HALO
        col = jnp.clip(corner_ref[1, k], -HALO, core + HALO - PATCH) + LANE
        tile = lax.shift_right_logical(col, 7)
        return row, tile, col - tile * LANE

    patches = count_ref[0]
    lanes = lax.broadcasted_iota(jnp.int32, (PATCH, LANE), 1)

    def place(k, plane, value, shift):
        late = lanes < shift
        first, second = (pltpu.roll(value[:, t * LANE : (t + 1) * LANE], shift, 1) for t in range(2))
        zero = jnp.zeros_like(first)
        parts = (jnp.where(late, zero, first), jnp.where(late, first, second), jnp.where(late, second, zero))
        for t, tile in enumerate(parts):
            placed[k, plane, t + 1, BLOCK : BLOCK + PATCH, :] = jnp.where(k < patches, tile, 0.0)

    def outward(k, carry):
        row, tile, shift = position(k)
        back = lax.rem(LANE - shift, LANE)
        early = lanes < LANE - shift

        def window(plane):
            turned = [pltpu.roll(ext_ref[plane, tile + t, pl.ds(row, PATCH), :], back, 1) for t in range(3)]
            return jnp.concatenate(
                [jnp.where(early, turned[0], turned[1]), jnp.where(early, turned[1], turned[2])], 1
            )

        pr, pi = probe_ref[0], probe_ref[1]
        hr, hi = prop_ref[0], prop_ref[1]
        ar, ai = window(0), window(1)
        sr, si = transform(stacked(pr * ar - pi * ai, pr * ai + pi * ar), fwd_ref[...], inv_ref[...])
        wr, wi = transform(stacked(hr * sr - hi * si, hr * si + hi * sr), inv_ref[...], fwd_ref[...])
        br, bi = window(2), window(3)
        fr, fi = transform(stacked(br * wr - bi * wi, br * wi + bi * wr), fwd_ref[...], inv_ref[...])
        level = fr * fr + fi * fi - measured_ref[k]
        gr, gi = transform(stacked(level * fr, level * fi), inv_ref[...], fwd_ref[...])
        place(k, 2, wr * gr + wi * gi, shift)
        place(k, 3, wr * gi - wi * gr, shift)
        through[k] = stacked(br * gr + bi * gi, br * gi - bi * gr)
        return carry

    def inward(k, carry):
        _, _, shift = position(k)
        pr, pi = probe_ref[0], probe_ref[1]
        hr, hi = prop_ref[0], prop_ref[1]
        tr, ti = transform(through[k], fwd_ref[...], inv_ref[...])
        qr, qi = transform(stacked(hr * tr + hi * ti, hr * ti - hi * tr), inv_ref[...], fwd_ref[...])
        place(k, 0, pr * qr + pi * qi, shift)
        place(k, 1, pr * qi - pi * qr, shift)
        return carry

    spots = [position(k)[:2] for k in range(PMAX)]

    def gathered(plane, tile, block):
        total = None
        for k, (row, first) in enumerate(spots):
            at = jnp.clip(block * BLOCK - row, -BLOCK, PATCH) + BLOCK
            value = placed[k, plane, jnp.clip(tile - first, -1, 3) + 1, pl.ds(at, BLOCK), :]
            total = value if total is None else total + value
        return total

    def fold_copy(side, slab, block):
        return remote(
            pack.at[side, slab, block], took.at[side, slab, block],
            fold_send.at[side, slab, block], fold_recv.at[side, slab, block], (r, c + (2 * side - 1), z),
        )

    def fold(slab):
        steps = (4, 3, -3, 2, -2, 1, -1, 0)
        for block in [0, blocks - 1] + [around(step) + 1 for step in steps]:
            for side, tile in ((0, 0), (1, 5)):
                for p in range(2):
                    whole = gathered(2 * slab + p, tile, block)
                    pack[side, slab, block, p] = whole[:half] + pltpu.roll(whole[half:], BLOCK, 1)
            pl.when(has_left)(lambda: fold_copy(0, slab, block).start())
            pl.when(has_right)(lambda: fold_copy(1, slab, block).start())

    def await_fold(slab, block):
        pl.when(has_right)(lambda: fold_copy(0, slab, block).wait_recv())
        pl.when(has_left)(lambda: fold_copy(1, slab, block).wait_recv())

    right_lanes = lax.broadcasted_iota(jnp.int32, (half, LANE), 1) >= BLOCK

    def local(block, slab, p, part):
        tiles = [gathered(2 * slab + p, 2 * part + 1 + t, block) for t in range(2)]
        side, edge = (1, 0) if part == 0 else (0, 1)
        packed = took[side, slab, block, p]
        turned = pltpu.roll(packed, BLOCK, 1)
        zero = jnp.zeros_like(packed)
        if part == 0:
            pieces = [jnp.where(right_lanes, zero, packed), jnp.where(right_lanes, zero, turned)]
        else:
            pieces = [jnp.where(right_lanes, packed, zero), jnp.where(right_lanes, turned, zero)]
        tiles[edge] = tiles[edge] + jnp.concatenate(pieces, 0)
        return tiles

    sent = []

    def rim_copy(chain, step, slab, source):
        return remote(
            source, rim_slot.at[chain, step, slab],
            rim_send.at[chain, step, slab], rim_recv.at[chain, step, slab], (r, c, around(CHAINS[chain][0])),
        )

    def main_copy(chain, step, slab, source):
        return remote(
            source, slot.at[chain, step, slab],
            main_send.at[chain, step, slab], main_recv.at[chain, step, slab], (r, c, around(CHAINS[chain][0])),
        )

    own = piece_rows(0, z)

    def rim_load(slab):
        for index, block in enumerate((0, blocks - 1)):
            await_fold(slab, block)
            for part in range(2):
                for p in range(2):
                    for t, tile in enumerate(local(block, slab, p, part)):
                        rim[part, slab, index, p, t] = tile

    def rim_round(k, slab):
        for chain, (direction, part, length) in enumerate(CHAINS):
            step = k - (FAR - length)
            if step < 0:
                continue
            piece = piece_rows(0, around(direction * (FAR - k)))
            if step == 0:
                source = rim.at[part, slab, :, :, :, piece, :]
            else:
                source = rim_slot.at[chain, step - 1, slab]
                rim_copy(chain, step - 1, slab, source).wait_recv()
                source[...] += rim[part, slab, :, :, :, piece, :]
            copy = rim_copy(chain, step, slab, source)
            copy.start()
            sent.append(copy)

    def main_round(k, slab):
        for offset in ((4,), (3, -3), (2, -2), (1, -1))[k]:
            await_fold(slab, around(offset) + 1)
        for chain, (direction, part, length) in enumerate(CHAINS):
            step = k - (FAR - length)
            if step < 0:
                continue
            block = around(direction * (FAR - k)) + 1
            if step == 0:
                source = stage.at[chain, slab]
            else:
                source = slot.at[chain, step - 1, slab]
                main_copy(chain, step - 1, slab, source).wait_recv()
            for p in range(2):
                for t, tile in enumerate(local(block, slab, p, part)):
                    if step == 0:
                        source[p, t] = tile
                    else:
                        source[p, t] += tile
            copy = main_copy(chain, step, slab, source)
            copy.start()
            sent.append(copy)

    def ends(part):
        return [(chain, length - 1) for chain, (_, q, length) in enumerate(CHAINS) if q == part]

    def far_copy(side, slab):
        target = (r - 1, c, last) if side == 0 else (r + 1, c, 0)
        return remote(
            rim_sum.at[slab, side], far.at[slab, :, :, own, :], far_send.at[slab, side], far_recv.at[slab, z], target
        )

    def rim_end(slab):
        for part in range(2):
            (a, i), (b, j) = ends(part)
            for chain, step in ((a, i), (b, j)):
                rim_copy(chain, step, slab, rim_slot.at[chain, step, slab]).wait_recv()
            total = rim[part, slab, :, :, :, own, :] + rim_slot[a, i, slab] + rim_slot[b, j, slab]
            rim_sum[slab, :, :, 2 * part : 2 * part + 2] = total
        pl.when(has_up)(lambda: far_copy(0, slab).start())
        pl.when(has_down)(lambda: far_copy(1, slab).start())

    takes = jnp.logical_or(jnp.logical_and(z == last, has_down), jnp.logical_and(z == 0, has_up))

    def finish(slab):
        await_fold(slab, z + 1)
        for part in range(2):
            (a, i), (b, j) = ends(part)
            for chain, step in ((a, i), (b, j)):
                main_copy(chain, step, slab, slot.at[chain, step, slab]).wait_recv()
            for p in range(2):
                tiles = local(z + 1, slab, p, part)
                for t in range(2):
                    out_ref[2 * slab + p, :, (2 * part + t) * LANE : (2 * part + t + 1) * LANE] = (
                        tiles[t] + slot[a, i, slab, p, t] + slot[b, j, slab, p, t]
                    )

        @pl.when(takes)
        def _():
            for other in range(depth):
                remote(
                    rim_sum.at[slab, 0], far.at[slab, :, :, other * PIECE : (other + 1) * PIECE, :],
                    far_send.at[slab, 0], far_recv.at[slab, other], (r, c, around(1)),
                ).wait_recv()
            for p in range(2):
                for t in range(4):
                    out_ref[2 * slab + p, :, t * LANE : (t + 1) * LANE] += far[slab, p, t]

    pl.when(jnp.logical_not(has_right))(lambda: took.__setitem__(0, jnp.zeros_like(took[0])))
    pl.when(jnp.logical_not(has_left))(lambda: took.__setitem__(1, jnp.zeros_like(took[1])))

    lax.fori_loop(0, PMAX, outward, 0)
    fold(1)
    rim_load(1)
    rim_round(0, 1)
    main_round(0, 1)
    lax.fori_loop(0, PMAX, inward, 0)
    fold(0)
    rim_round(1, 1)
    rim_load(0)
    rim_round(0, 0)
    main_round(0, 0)
    rim_round(2, 1)
    main_round(1, 1)
    rim_round(1, 0)
    rim_round(3, 1)
    rim_round(2, 0)
    main_round(1, 0)
    rim_end(1)
    rim_round(3, 0)
    main_round(2, 1)
    rim_end(0)
    main_round(2, 0)
    main_round(3, 1)
    main_round(3, 0)
    finish(1)
    finish(0)

    for copy in sent:
        copy.wait_send()
    for slab in range(2):
        pl.when(has_up)(lambda: far_copy(0, slab).wait_send())
        pl.when(has_down)(lambda: far_copy(1, slab).wait_send())
    for side in range(2):

        @pl.when((has_left, has_right)[side])
        def _():
            for slab in range(2):
                for block in range(blocks):
                    fold_copy(side, slab, block).wait_send()
            side_copy(1 - side).wait_send()

        @pl.when((has_down, has_up)[side])
        def _():
            row_copy(side).wait_send()

        @pl.when(live[side])
        def _():
            for at, part, offset, index in corners:
                if at == side:
                    pl.when(targets[part][0])(lambda: corner_copy(side, part, offset, index).wait_send())
            for chain, (_, _, length) in enumerate(CHAINS):
                for step in range(length):
                    ring_copy(side, chain, step).wait_send()


def fused_call(sizes, count, corners, field, phase, probe, halves, measured):
    planes, core, _ = field.shape
    depth = sizes[2]
    reach = core + 2 * HALO
    blocks = reach // BLOCK
    f32, bf16 = jnp.float32, jnp.bfloat16
    dma = pltpu.SemaphoreType.DMA
    smem = pl.BlockSpec(memory_space=pltpu.SMEM)
    return pl.pallas_call(
        functools.partial(fused_kernel, sizes),
        out_shape=jax.ShapeDtypeStruct((planes, BLOCK, core), f32),
        in_specs=[smem, smem] + [pl.BlockSpec(memory_space=pltpu.HBM)] * 5,
        out_specs=pl.BlockSpec(memory_space=pltpu.VMEM),
        scratch_shapes=[
            pltpu.VMEM((planes, 6, reach, LANE), f32),
            pltpu.VMEM((2, PATCH, PATCH), f32),
            pltpu.VMEM((2, PATCH, PATCH), f32),
            pltpu.VMEM((PMAX, PATCH, PATCH), f32),
            pltpu.VMEM((2 * PATCH, 2 * PATCH), bf16),
            pltpu.VMEM((2 * PATCH, 2 * PATCH), bf16),
            pltpu.VMEM((2, PATCH, PATCH), bf16),
            pltpu.VMEM((PMAX, 2 * PATCH, PATCH), bf16),
            pltpu.VMEM((PMAX, planes, 5, PATCH + 2 * BLOCK, LANE), f32),
            pltpu.VMEM((2, 2, blocks, 2, BLOCK // 2, LANE), f32),
            pltpu.VMEM((2, 2, blocks, 2, BLOCK // 2, LANE), f32),
            pltpu.VMEM((4, 2, 2, 2, BLOCK, LANE), f32),
            pltpu.VMEM((2, 2, 2, 2, 2, BLOCK, LANE), f32),
            pltpu.VMEM((4, FAR, 2, 2, 2, 2, PIECE, LANE), f32),
            pltpu.VMEM((4, FAR, 2, 2, 2, BLOCK, LANE), f32),
            pltpu.VMEM((2, 2, 2, 4, PIECE, LANE), f32),
            pltpu.VMEM((2, 2, 4, BLOCK, LANE), f32),
            dma((4,)), dma((4,)), dma((2,)), dma((2,)), dma((2, 4, FAR)), dma((2, 4, FAR)),
            dma((2,)), dma((2,)), dma((2, 2, depth)), dma((2, 2, depth)),
            dma((2, 2, blocks)), dma((2, 2, blocks)), dma((4, FAR, 2)), dma((4, FAR, 2)),
            dma((4, FAR, 2)), dma((4, FAR, 2)), dma((2, 2)), dma((2, depth)),
        ],
        compiler_params=pltpu.CompilerParams(
            collective_id=0, has_side_effects=True, vmem_limit_bytes=63 << 20
        ),
    )(count, corners, field, phase, probe, halves, measured)


def shards(sizes, object_field, probe_field, prop_phase, measured, positions, counts):
    gradient = fused_call(
        sizes,
        counts.reshape(1),
        positions.reshape(PMAX, 2).T,
        object_field.reshape(4, *object_field.shape[2:]),
        prop_phase,
        probe_field,
        jnp.asarray(dft_halves()),
        measured.reshape(PMAX, PATCH, PATCH),
    )
    return gradient.reshape(2, 2, *gradient.shape[1:])


def solution(mesh):
    placed = (
        P(None, None, "row", "col"),
        P(),
        P(),
        P("row", "col", "scan", None, None, None),
        P("row", "col", "scan", None, None),
        P("row", "col", "scan"),
    )
    sizes = tuple(mesh.shape[name] for name in ("row", "col", "scan"))
    return jax.shard_map(
        functools.partial(shards, sizes),
        mesh=mesh,
        in_specs=placed,
        out_specs=P(None, None, ("row", "scan"), "col"),
        check_vma=False,
    )
```

time: 415 us -> 120 us (0.29)
  waiting for transfers between devices: 150 us -> 0 us
  starting transfers between devices: 147 us -> 0 us
  Pallas kernels: 0 us -> 116 us
  local copies, waits for them, and re-layouts: 67.6 us -> 1.87 us
  other arithmetic: 27 us -> 0 us
  between operations: 14.3 us -> 0.66 us
    ppermute x8 -> x0, starting transfers between devices: 147 us -> none  [the longest x4 120 us: from_behind(): return lax.ppermute(block, axis, route)]
    pallas_call x0 -> x1, Pallas kernels: none -> 116 us  [fused_call(): pl.pallas_call(functools.partial(fused_kernel, sizes), out_shape=jax.Shap...]
    unnamed x2 -> x0, waiting for transfers between devices: 108 us -> none
    ppermute x8 -> x0, waiting for transfers between devices: 41.2 us -> none  [the longest x2 23.6 us: extended_2(): after = lax.ppermute(first, axis, down)]
    scatter-add x3 -> x0, local copies, waits for them, and re-layouts: 18.4 us -> none  [the longest x2 12.6 us: fold_cols(): return core_cols.at[:, :, tile_size - HALO:].add(pass_cols(left_rim, -1))]
    slice x8 -> x0, local copies, waits for them, and re-layouts: 13.5 us -> none  [the longest x1 5.68 us: fold_cols(): core_cols = gradient[:, :, HALO:tile_size + HALO]]
    dynamic_update_slice x2 -> x0, local copies, waits for them, and re-layouts: 12.4 us -> none  [add_patch(): return lax.dynamic_update_slice(current, present + update, starts)]
    another operation x11 -> x0, other arithmetic: 10.5 us -> none
  transfers between devices with their start and end apart: 9 -> 0, of which waited for: 6 -> 0; matrix products, arithmetic and copies ran while one was open for 8% -> 0% of each run, Pallas kernels for 0% -> 0%
where the time goes in v2:
time: 120 us; the launch traced here: 119 us
  Pallas kernels  116 us (97%)
  local copies, waits for them, and re-layouts  1.87 us (2%)
    pallas_call x1, Pallas kernels, fused_call(): pl.pallas_call(functools.partial(fused_kernel, sizes), out_shape=jax.Shap...  116 us

profile of v2, /device:TPU:1, one launch (start us, length us, event | category | flops | bytes accessed | tf_op | source)
XLA Modules:
  0.0 118.9 jit_solution(6938159651301911701)
XLA Ops:
  0.7 116.3 %shard_map.73 = f32[4,64,512]{2,1,0:T(8,128)} custom-call(s32[1]{0:T(128)} %bitcast.7.count_ref, s32[2,3]{1,0:T(2,128)} %bitcast.11, f32[4,512,512]{2,1,0:T(8,128)} %bitcast.8, f32[256,256]{1,0:T(8,128)} %phase_ref.1, f32[2,256,256]{2,1,0:T(8,128)} %probe_hbm.1, bf16[2,256,256]{2,1,0:T(8,128)(2,1)} %constant.2.clone.half_ref, f32[3,256,256]{2,1,0:T(8,128)} %bitcast.10), custom_call_target="tpu_custom_call" | custom-call | tf_op jit(solution)/shard_map/pallas_call | solution.py:460
  117.0 1.9 %copy.10 = f32[2,2,64,512]{3,2,1,0:T(8,128)} copy(f32[2,2,64,512]{3,2,1,0:T(8,128)} %bitcast.9) | data formatting | bytes 1048576

commit v3 on v2

--- a/solution.py
+++ b/solution.py
@@ -31,11 +31,12 @@
     return jnp.concatenate([real.astype(jnp.bfloat16), imag.astype(jnp.bfloat16)], 0)
 
 
-def transform(rows, left, right):
-    middle = jnp.dot(left, rows, preferred_element_type=jnp.float32).astype(jnp.bfloat16)
-    middle = jnp.concatenate([middle[:PATCH], middle[PATCH:]], 1)
-    out = jnp.dot(middle, right, preferred_element_type=jnp.float32)
-    return out[:, :PATCH], out[:, PATCH:]
+def transform(batch, left, right):
+    middle = jnp.dot(left, jnp.concatenate(batch, 1), preferred_element_type=jnp.float32).astype(jnp.bfloat16)
+    spans = [slice(k * PATCH, (k + 1) * PATCH) for k in range(len(batch))]
+    wide = jnp.concatenate([jnp.concatenate([middle[:PATCH, at], middle[PATCH:, at]], 1) for at in spans], 0)
+    out = jnp.dot(wide, right, preferred_element_type=jnp.float32)
+    return [(out[at, :PATCH], out[at, PATCH:]) for at in spans]
 
 
 def fused_kernel(
@@ -203,40 +204,50 @@
         for t, tile in enumerate(parts):
             placed[k, plane, t + 1, BLOCK : BLOCK + PATCH, :] = jnp.where(k < patches, tile, 0.0)
 
-    def outward(k, carry):
+    def window(k, plane):
         row, tile, shift = position(k)
         back = lax.rem(LANE - shift, LANE)
         early = lanes < LANE - shift
-
-        def window(plane):
-            turned = [pltpu.roll(ext_ref[plane, tile + t, pl.ds(row, PATCH), :], back, 1) for t in range(3)]
-            return jnp.concatenate(
-                [jnp.where(early, turned[0], turned[1]), jnp.where(early, turned[1], turned[2])], 1
-            )
-
+        turned = [pltpu.roll(ext_ref[plane, tile + t, pl.ds(row, PATCH), :], back, 1) for t in range(3)]
+        return jnp.concatenate([jnp.where(early, turned[0], turned[1]), jnp.where(early, turned[1], turned[2])], 1)
+
+    def forward(batch):
+        return transform(batch, fwd_ref[...], inv_ref[...])
+
+    def inverse(batch):
+        return transform(batch, inv_ref[...], fwd_ref[...])
+
+    def outward():
         pr, pi = probe_ref[0], probe_ref[1]
         hr, hi = prop_ref[0], prop_ref[1]
-        ar, ai = window(0), window(1)
-        sr, si = transform(stacked(pr * ar - pi * ai, pr * ai + pi * ar), fwd_ref[...], inv_ref[...])
-        wr, wi = transform(stacked(hr * sr - hi * si, hr * si + hi * sr), inv_ref[...], fwd_ref[...])
-        br, bi = window(2), window(3)
-        fr, fi = transform(stacked(br * wr - bi * wi, br * wi + bi * wr), fwd_ref[...], inv_ref[...])
-        level = fr * fr + fi * fi - measured_ref[k]
-        gr, gi = transform(stacked(level * fr, level * fi), inv_ref[...], fwd_ref[...])
-        place(k, 2, wr * gr + wi * gi, shift)
-        place(k, 3, wr * gi - wi * gr, shift)
-        through[k] = stacked(br * gr + bi * gi, br * gi - bi * gr)
-        return carry
-
-    def inward(k, carry):
-        _, _, shift = position(k)
+        batch = []
+        for k in range(PMAX):
+            ar, ai = window(k, 0), window(k, 1)
+            batch.append(stacked(pr * ar - pi * ai, pr * ai + pi * ar))
+        arrived = inverse([stacked(hr * sr - hi * si, hr * si + hi * sr) for sr, si in forward(batch)])
+        batch = []
+        for k, (wr, wi) in enumerate(arrived):
+            br, bi = window(k, 2), window(k, 3)
+            batch.append(stacked(br * wr - bi * wi, br * wi + bi * wr))
+        batch, distant = [], forward(batch)
+        for k, (fr, fi) in enumerate(distant):
+            level = fr * fr + fi * fi - measured_ref[k]
+            batch.append(stacked(level * fr, level * fi))
+        for k, ((wr, wi), (gr, gi)) in enumerate(zip(arrived, inverse(batch), strict=True)):
+            shift = position(k)[2]
+            br, bi = window(k, 2), window(k, 3)
+            place(k, 2, wr * gr + wi * gi, shift)
+            place(k, 3, wr * gi - wi * gr, shift)
+            through[k] = stacked(br * gr + bi * gi, br * gi - bi * gr)
+
+    def inward():
         pr, pi = probe_ref[0], probe_ref[1]
         hr, hi = prop_ref[0], prop_ref[1]
-        tr, ti = transform(through[k], fwd_ref[...], inv_ref[...])
-        qr, qi = transform(stacked(hr * tr + hi * ti, hr * ti - hi * tr), inv_ref[...], fwd_ref[...])
-        place(k, 0, pr * qr + pi * qi, shift)
-        place(k, 1, pr * qi - pi * qr, shift)
-        return carry
+        spectra = forward([through[k] for k in range(PMAX)])
+        for k, (qr, qi) in enumerate(inverse([stacked(hr * tr + hi * ti, hr * ti - hi * tr) for tr, ti in spectra])):
+            shift = position(k)[2]
+            place(k, 0, pr * qr + pi * qi, shift)
+            place(k, 1, pr * qi - pi * qr, shift)
 
     spots = [position(k)[:2] for k in range(PMAX)]
 
@@ -394,26 +405,26 @@
     pl.when(jnp.logical_not(has_right))(lambda: took.__setitem__(0, jnp.zeros_like(took[0])))
     pl.when(jnp.logical_not(has_left))(lambda: took.__setitem__(1, jnp.zeros_like(took[1])))
 
-    lax.fori_loop(0, PMAX, outward, 0)
+    outward()
     fold(1)
+    inward()
+    fold(0)
     rim_load(1)
     rim_round(0, 1)
     main_round(0, 1)
-    lax.fori_loop(0, PMAX, inward, 0)
-    fold(0)
-    rim_round(1, 1)
     rim_load(0)
     rim_round(0, 0)
     main_round(0, 0)
+    rim_round(1, 1)
+    rim_round(1, 0)
+    main_round(1, 1)
     rim_round(2, 1)
-    main_round(1, 1)
-    rim_round(1, 0)
-    rim_round(3, 1)
     rim_round(2, 0)
     main_round(1, 0)
-    rim_end(1)
+    rim_round(3, 1)
     rim_round(3, 0)
     main_round(2, 1)
+    rim_end(1)
     rim_end(0)
     main_round(2, 0)
     main_round(3, 1)

time: 120 us -> 115 us (0.958)
  Pallas kernels: 116 us -> 111 us
    pallas_call x1, Pallas kernels: 116 us -> 111 us  [fused_call(): pl.pallas_call(functools.partial(fused_kernel, sizes), out_shape=jax.Shap...]
where the time goes in v3:
time: 115 us; the launch traced here: 113 us
  Pallas kernels  111 us (97%)
  local copies, waits for them, and re-layouts  1.87 us (2%)
    pallas_call x1, Pallas kernels, fused_call(): pl.pallas_call(functools.partial(fused_kernel, sizes), out_shape=jax.Shap...  111 us

profile of v3, /device:TPU:1, one launch (start us, length us, event | category | flops | bytes accessed | tf_op | source)
XLA Modules:
  0.0 113.1 jit_solution(16777671147005615208)
XLA Ops:
  0.7 110.6 %shard_map.73 = f32[4,64,512]{2,1,0:T(8,128)} custom-call(s32[1]{0:T(128)} %bitcast.7.count_ref, s32[2,3]{1,0:T(2,128)} %bitcast.11, f32[4,512,512]{2,1,0:T(8,128)} %bitcast.8, f32[256,256]{1,0:T(8,128)} %phase_ref.1, f32[2,256,256]{2,1,0:T(8,128)} %probe_hbm.1, bf16[2,256,256]{2,1,0:T(8,128)(2,1)} %constant.2.clone.half_ref, f32[3,256,256]{2,1,0:T(8,128)} %bitcast.10), custom_call_target="tpu_custom_call" | custom-call | tf_op jit(solution)/shard_map/pallas_call | solution.py:471
  111.3 1.9 %copy.10 = f32[2,2,64,512]{3,2,1,0:T(8,128)} copy(f32[2,2,64,512]{3,2,1,0:T(8,128)} %bitcast.9) | data formatting | bytes 1048576

commit v4 on v3

--- a/solution.py
+++ b/solution.py
@@ -17,6 +17,7 @@
 PIECE = 8
 FAR = 4
 CHAINS = ((1, 0, 3), (1, 1, 4), (-1, 0, 4), (-1, 1, 3))
+WAYS = (1, -1)
 MESH = pl.DeviceIdType.MESH
 
 
@@ -41,7 +42,7 @@
 
 def fused_kernel(
     sizes, count_ref, corner_ref, field_ref, phase_ref, probe_hbm, half_ref, measured_hbm, out_ref,
-    ext_ref, prop_ref, probe_ref, measured_ref, fwd_ref, inv_ref, halves, through, placed,
+    ext_first, ext_second, prop_ref, probe_ref, measured_ref, fwd_ref, inv_ref, halves, through, placed,
     pack, took, stage, rim, rim_slot, slot, rim_sum, far,
     load_sem, core_sem, row_send, row_recv, ring_send, ring_recv, side_send, side_recv, corner_send, corner_recv,
     fold_send, fold_recv, rim_send, rim_recv, main_send, main_recv, far_send, far_recv,
@@ -52,7 +53,8 @@
     has_left, has_right = c > 0, c < cols - 1
     has_up, has_down = r > 0, r < rows - 1
     core = field_ref.shape[1]
-    blocks = ext_ref.shape[2] // BLOCK
+    exts = (ext_first, ext_second)
+    blocks = ext_first.shape[2] // BLOCK
     half = BLOCK // 2
 
     def around(step):
@@ -77,8 +79,11 @@
 
     fills = [
         pltpu.make_async_copy(
-            field_ref.at[:, :, t * LANE : (t + 1) * LANE], ext_ref.at[:, t + 1, HALO : HALO + core, :], core_sem.at[t]
-        )
+            field_ref.at[2 * slab : 2 * slab + 2, :, t * LANE : (t + 1) * LANE],
+            exts[slab].at[:, t + 1, HALO : HALO + core, :],
+            core_sem.at[slab, t],
+        )
+        for slab in range(2)
         for t in range(4)
     ]
     for fill in fills:
@@ -99,37 +104,42 @@
 
     starts = (0, HALO + core)
 
-    def row_copy(side):
+    def row_copy(side, slab):
         source = piece_rows(core if side == 0 else HALO, z)
         return remote(
-            ext_ref.at[:, 1:5, source, :], ext_ref.at[:, 1:5, piece_rows(starts[side], z), :],
-            row_send.at[side], row_recv.at[side], (r + 1 - 2 * side, c, z),
-        )
-
-    def side_copy(side):
+            exts[slab].at[:, 1:5, source, :],
+            exts[slab].at[:, 1:5, piece_rows(starts[side], z), :],
+            row_send.at[side, slab], row_recv.at[side, slab], (r + 1 - 2 * side, c, z),
+        )
+
+    def side_copy(side, slab):
         tile, target = ((4, 0), (1, 5))[side]
         return remote(
-            ext_ref.at[:, tile, HALO : HALO + core, :], ext_ref.at[:, target, HALO : HALO + core, :],
-            side_send.at[side], side_recv.at[side], (r, c + 1 - 2 * side, z),
-        )
-
-    def ring_copy(side, chain, step):
+            exts[slab].at[:, tile, HALO : HALO + core, :],
+            exts[slab].at[:, target, HALO : HALO + core, :],
+            side_send.at[side, slab], side_recv.at[side, slab], (r, c + 1 - 2 * side, z),
+        )
+
+    def ring_copy(side, chain, step, slab):
         direction, part, _ = CHAINS[chain]
-        place = ext_ref.at[:, 2 * part + 1 : 2 * part + 3, piece_rows(starts[side], around(-direction * step)), :]
-        return remote(
-            place, place, ring_send.at[side, chain, step], ring_recv.at[side, chain, step], (r, c, around(direction))
-        )
-
-    def corner_copy(side, part, offset, index):
+        rows_at = piece_rows(starts[side], around(-direction * step))
+        place = exts[slab].at[:, 2 * part + 1 : 2 * part + 3, rows_at, :]
+        return remote(
+            place, place,
+            ring_send.at[side, chain, step, slab], ring_recv.at[side, chain, step, slab], (r, c, around(direction)),
+        )
+
+    def corner_copy(side, part, offset, index, slab):
         tile, target = ((1, 5), (4, 0))[part]
-        place = piece_rows(starts[side], around(offset))
-        return remote(
-            ext_ref.at[:, tile, place, :], ext_ref.at[:, target, place, :],
-            corner_send.at[side, part, index], corner_recv.at[side, part, index], (r, c + 2 * part - 1, z),
-        )
-
-    pl.when(has_down)(lambda: row_copy(0).start())
-    pl.when(has_up)(lambda: row_copy(1).start())
+        rows_at = piece_rows(starts[side], around(offset))
+        return remote(
+            exts[slab].at[:, tile, rows_at, :], exts[slab].at[:, target, rows_at, :],
+            corner_send.at[side, part, index, slab], corner_recv.at[side, part, index, slab], (r, c + 2 * part - 1, z),
+        )
+
+    for slab in range(2):
+        pl.when(has_down)(lambda: row_copy(0, slab).start())
+        pl.when(has_up)(lambda: row_copy(1, slab).start())
 
     loads[0].wait()
     phase = prop_ref[0]
@@ -147,45 +157,56 @@
     live = (has_up, has_down)
     corners = []
 
-    def send_corner(side, part, offset):
-        index = len([1 for entry in corners if entry[:2] == (side, part)])
-        corners.append((side, part, offset, index))
-        pl.when(targets[part][0])(lambda: corner_copy(side, part, offset, index).start())
-
-    for step in range(FAR + 1):
+    def send_corner(side, part, offset, slab):
+        index = len([1 for entry in corners if entry[:2] == (side, part) and entry[4] == slab])
+        corners.append((side, part, offset, index, slab))
+        pl.when(targets[part][0])(lambda: corner_copy(side, part, offset, index, slab).start())
+
+    def ring_step(step, slab):
         for side in range(2):
 
             @pl.when(live[side])
             def _():
                 if step == 0:
-                    row_copy(side).wait_recv()
+                    row_copy(side, slab).wait_recv()
                 for chain, (direction, part, length) in enumerate(CHAINS):
                     if 0 < step <= length:
-                        ring_copy(side, chain, step - 1).wait_recv()
+                        ring_copy(side, chain, step - 1, slab).wait_recv()
                     if step < length:
-                        ring_copy(side, chain, step).start()
+                        ring_copy(side, chain, step, slab).start()
                 for chain, (direction, part, length) in enumerate(CHAINS):
                     if step == 0 and chain < 2:
-                        send_corner(side, chain, 0)
+                        send_corner(side, chain, 0, slab)
                     if 0 < step <= length:
-                        send_corner(side, part, -direction * step)
+                        send_corner(side, part, -direction * step, slab)
 
         if step == 0:
-            pl.when(has_right)(lambda: side_copy(0).start())
-            pl.when(has_left)(lambda: side_copy(1).start())
-            placed[...] = jnp.zeros_like(placed)
-
-    for side in range(2):
-        pl.when((has_left, has_right)[side])(lambda: side_copy(side).wait_recv())
-
-        @pl.when(live[side])
-        def _():
-            for at, part, offset, index in corners:
-                if at == side:
-                    pl.when(targets[part][1])(lambda: corner_copy(side, part, offset, index).wait_recv())
-
+            pl.when(has_right)(lambda: side_copy(0, slab).start())
+            pl.when(has_left)(lambda: side_copy(1, slab).start())
+
+    def await_halo(slab):
+        for side in range(2):
+            pl.when((has_left, has_right)[side])(lambda: side_copy(side, slab).wait_recv())
+
+            @pl.when(live[side])
+            def _():
+                for at, part, offset, index, which in corners:
+                    if at == side and which == slab:
+                        pl.when(targets[part][1])(lambda: corner_copy(side, part, offset, index, slab).wait_recv())
+
+    ring_step(0, 0)
+    placed[...] = jnp.zeros_like(placed)
+    ring_step(0, 1)
+    ring_step(1, 0)
+    ring_step(2, 0)
+    ring_step(1, 1)
+    ring_step(3, 0)
+    ring_step(2, 1)
+    ring_step(4, 0)
+    ring_step(3, 1)
     for load in loads[2:]:
         load.wait()
+    await_halo(0)
 
     def position(k):
         row = jnp.clip(corner_ref[0, k], -HALO, core + HALO - PATCH) + HALO
@@ -208,7 +229,7 @@
         row, tile, shift = position(k)
         back = lax.rem(LANE - shift, LANE)
         early = lanes < LANE - shift
-        turned = [pltpu.roll(ext_ref[plane, tile + t, pl.ds(row, PATCH), :], back, 1) for t in range(3)]
+        turned = [pltpu.roll(exts[plane // 2][plane % 2, tile + t, pl.ds(row, PATCH), :], back, 1) for t in range(3)]
         return jnp.concatenate([jnp.where(early, turned[0], turned[1]), jnp.where(early, turned[1], turned[2])], 1)
 
     def forward(batch):
@@ -224,7 +245,10 @@
         for k in range(PMAX):
             ar, ai = window(k, 0), window(k, 1)
             batch.append(stacked(pr * ar - pi * ai, pr * ai + pi * ar))
-        arrived = inverse([stacked(hr * sr - hi * si, hr * si + hi * sr) for sr, si in forward(batch)])
+        spectra = forward(batch)
+        ring_step(4, 1)
+        arrived = inverse([stacked(hr * sr - hi * si, hr * si + hi * sr) for sr, si in spectra])
+        await_halo(1)
         batch = []
         for k, (wr, wi) in enumerate(arrived):
             br, bi = window(k, 2), window(k, 3)
@@ -444,20 +468,23 @@
             for slab in range(2):
                 for block in range(blocks):
                     fold_copy(side, slab, block).wait_send()
-            side_copy(1 - side).wait_send()
+            for slab in range(2):
+                side_copy(1 - side, slab).wait_send()
 
         @pl.when((has_down, has_up)[side])
         def _():
-            row_copy(side).wait_send()
+            for slab in range(2):
+                row_copy(side, slab).wait_send()
 
         @pl.when(live[side])
         def _():
-            for at, part, offset, index in corners:
+            for at, part, offset, index, slab in corners:
                 if at == side:
-                    pl.when(targets[part][0])(lambda: corner_copy(side, part, offset, index).wait_send())
+                    pl.when(targets[part][0])(lambda: corner_copy(side, part, offset, index, slab).wait_send())
             for chain, (_, _, length) in enumerate(CHAINS):
                 for step in range(length):
-                    ring_copy(side, chain, step).wait_send()
+                    for slab in range(2):
+                        ring_copy(side, chain, step, slab).wait_send()
 
 
 def fused_call(sizes, count, corners, field, phase, probe, halves, measured):
@@ -474,7 +501,8 @@
         in_specs=[smem, smem] + [pl.BlockSpec(memory_space=pltpu.HBM)] * 5,
         out_specs=pl.BlockSpec(memory_space=pltpu.VMEM),
         scratch_shapes=[
-            pltpu.VMEM((planes, 6, reach, LANE), f32),
+            pltpu.VMEM((planes // 2, 6, reach, LANE), f32),
+            pltpu.VMEM((planes // 2, 6, reach, LANE), f32),
             pltpu.VMEM((2, PATCH, PATCH), f32),
             pltpu.VMEM((2, PATCH, PATCH), f32),
             pltpu.VMEM((PMAX, PATCH, PATCH), f32),
@@ -491,8 +519,8 @@
             pltpu.VMEM((4, FAR, 2, 2, 2, BLOCK, LANE), f32),
             pltpu.VMEM((2, 2, 2, 4, PIECE, LANE), f32),
             pltpu.VMEM((2, 2, 4, BLOCK, LANE), f32),
-            dma((4,)), dma((4,)), dma((2,)), dma((2,)), dma((2, 4, FAR)), dma((2, 4, FAR)),
-            dma((2,)), dma((2,)), dma((2, 2, depth)), dma((2, 2, depth)),
+            dma((4,)), dma((2, 4)), dma((2, 2)), dma((2, 2)), dma((2, 4, FAR, 2)), dma((2, 4, FAR, 2)),
+            dma((2, 2)), dma((2, 2)), dma((2, 2, depth, 2)), dma((2, 2, depth, 2)),
             dma((2, 2, blocks)), dma((2, 2, blocks)), dma((4, FAR, 2)), dma((4, FAR, 2)),
             dma((4, FAR, 2)), dma((4, FAR, 2)), dma((2, 2)), dma((2, depth)),
         ],

time: 115 us -> 117 us (1.017)
  the two profiles are of different devices: /device:TPU:1 before, /device:TPU:5 now
where the time goes in v4:
time: 117 us
  Pallas kernels  114 us (97%)
  local copies, waits for them, and re-layouts  1.87 us (2%)
    pallas_call x1, Pallas kernels, fused_call(): pl.pallas_call(functools.partial(fused_kernel, sizes), out_shape=jax.Shap...  114 us

profile of v4, /device:TPU:5, one launch (start us, length us, event | category | flops | bytes accessed | tf_op | source)
XLA Modules:
  0.0 116.9 jit_solution(6804704306775125845)
XLA Ops:
  0.7 114.4 %shard_map.73 = f32[4,64,512]{2,1,0:T(8,128)} custom-call(s32[1]{0:T(128)} %bitcast.7.count_ref, s32[2,3]{1,0:T(2,128)} %bitcast.11, f32[4,512,512]{2,1,0:T(8,128)} %bitcast.8, f32[256,256]{1,0:T(8,128)} %phase_ref.1, f32[2,256,256]{2,1,0:T(8,128)} %probe_hbm.1, bf16[2,256,256]{2,1,0:T(8,128)(2,1)} %constant.2.clone.half_ref, f32[3,256,256]{2,1,0:T(8,128)} %bitcast.10), custom_call_target="tpu_custom_call" | custom-call | tf_op jit(solution)/shard_map/pallas_call | solution.py:498
  115.0 1.9 %copy.10 = f32[2,2,64,512]{3,2,1,0:T(8,128)} copy(f32[2,2,64,512]{3,2,1,0:T(8,128)} %bitcast.9) | data formatting | bytes 1048576
